TPU v7x, 256 devices: a whole 4x4x8 slice. The times are simulated.
256 devices in a mesh: seq: 32 (over z, y), dp: 8 (over x, core).
Axes of the slice: x: 4, y: 4, z: 8, core: 2. Of those that a mesh axis runs over, the one named last changes fastest.
Arguments:
- queries: bfloat16 [8, 4096, 4096], P('dp', 'seq'), may hold values from -118 to 118
- keys: bfloat16 [8, 4096, 1024], P('dp', 'seq'), may hold values from -9 to 9
- hidden: bfloat16 [8, 4096, 4096], P('dp', 'seq'), may hold values from -6 to 6
- value_weight: bfloat16 [4096, 1024], P('dp'), may hold values from -0.09375 to 0.09375
- readout: bfloat16 [4096, 256], replicated, may hold values from -1.796875 to 1.796875
- base_logits: float32 [8, 4096, 256], P('dp', 'seq'), may hold values from -12 to 300
- labels: int32 [8, 4096], P('dp', 'seq'), may hold values from 0 to 255
- hessian: float32 [1024, 4096], P('seq', 'dp'), may hold values from 0.05 to 2
Outputs:
- estimate: float32 [1024, 4096], P('seq', 'dp')
- hessian_new: float32 [1024, 4096], P('seq', 'dp')
All inputs are finite; a program needn't handle non-finite values.
Results may differ from a plain program's by a relative error of at most 0.033.
Values may be sent and summed in bfloat16 or wider, within the bound.
A program may use at most 64 MiB of HBM per device.

v0:
```python
import math

import jax
import jax.numpy as jnp
from jax import lax
from jax.sharding import PartitionSpec as P

HD = 128


big_negative = -1e30
beta_two = 0.99


def in_blocks(x, dim, count):
    before, after = (x.shape[:dim], x.shape[dim + 1 :])
    return jnp.moveaxis(x.reshape(*before, count, -1, *after), dim, 0)


def sum_at_owner(x, axis, dim):
    blocks = in_blocks(x, dim, lax.axis_size(axis))
    arrived = lax.all_to_all(blocks, axis, split_axis=0, concat_axis=0, tiled=True)
    return arrived.astype(jnp.float32).sum(axis=0)


def cut_rows(length, count):
    turn = length // count
    if turn >= 8:
        turn -= turn % 8
    return [turn * k for k in range(1, count)]


def in_order(blocks, dim):
    shape = list(blocks.shape[1:])
    shape[dim] *= blocks.shape[0]
    return jnp.moveaxis(blocks, 0, dim).reshape(shape)


def several_exchanges(x, axis, pieces, split_dim, concat_dim):
    blocks = in_blocks(x, split_dim, lax.axis_size(axis))
    cut = max(range(1, max(2, blocks.ndim - 1)), key=lambda d: blocks.shape[d])
    done = []
    for share in jnp.split(blocks, cut_rows(blocks.shape[cut], pieces), axis=cut):
        if share.size:
            done.append(lax.all_to_all(share, axis, split_axis=0, concat_axis=0, tiled=True))
    return in_order(jnp.concatenate(done, axis=cut), concat_dim)


def sent_to_all(x, axis):
    copies = jnp.broadcast_to(x, (lax.axis_size(axis), *x.shape))
    return lax.all_to_all(copies, axis, split_axis=0, concat_axis=0, tiled=True)


def collect(x, axis, dim):
    return in_order(sent_to_all(x, axis), dim)


def block_scores(q_block, k_block, row_start, col_start, scale):
    scores = (
        jnp.einsum("hqd,hkd->hqk", q_block, k_block, preferred_element_type=jnp.float32) * scale
    )
    rows_pos = row_start + lax.broadcasted_iota(jnp.int32, scores.shape, 1)
    cols_pos = col_start + lax.broadcasted_iota(jnp.int32, scores.shape, 2)
    return jnp.where(cols_pos <= rows_pos, scores, big_negative)


def row_statistics(queries, keys, width, scale):
    heads, length, _ = queries.shape
    blocks = length // width

    def row_outer(i, state):
        i = jnp.asarray(i).astype(jnp.int32)
        peak_all, total_all = state
        q_block = lax.dynamic_slice_in_dim(queries, i * width, width, 1)

        def row_inner(j, carry):
            j = jnp.asarray(j).astype(jnp.int32)
            peak, total = carry
            k_block = lax.dynamic_slice_in_dim(keys, j * width, width, 1)
            scores = block_scores(q_block, k_block, i * width, j * width, scale)
            fresh = jnp.maximum(peak, jnp.max(scores, axis=2))
            total = total * jnp.exp(peak - fresh) + jnp.sum(
                jnp.exp(scores - fresh[:, :, None]), axis=2
            )
            return (fresh, total)

        starting = (
            jnp.full((heads, width), big_negative, jnp.float32),
            jnp.zeros((heads, width), jnp.float32),
        )
        peak, total = lax.fori_loop(0, i + 1, row_inner, starting)
        peak_all = lax.dynamic_update_slice_in_dim(peak_all, peak, i * width, 1)
        total_all = lax.dynamic_update_slice_in_dim(total_all, total, i * width, 1)
        return (peak_all, total_all)

    starting = (jnp.zeros((heads, length), jnp.float32), jnp.zeros((heads, length), jnp.float32))
    return lax.fori_loop(0, blocks, row_outer, starting)


def attend(queries, keys, values, peak, total, width, scale):
    heads, length, dim = queries.shape
    blocks = length // width

    def attend_outer(i, output):
        i = jnp.asarray(i).astype(jnp.int32)
        q_block = lax.dynamic_slice_in_dim(queries, i * width, width, 1)
        peak_block = lax.dynamic_slice_in_dim(peak, i * width, width, 1)
        total_block = lax.dynamic_slice_in_dim(total, i * width, width, 1)

        def attend_inner(j, running):
            j = jnp.asarray(j).astype(jnp.int32)
            k_block = lax.dynamic_slice_in_dim(keys, j * width, width, 1)
            v_block = lax.dynamic_slice_in_dim(values, j * width, width, 1)
            scores = block_scores(q_block, k_block, i * width, j * width, scale)
            weights = (jnp.exp(scores - peak_block[:, :, None]) / total_block[:, :, None]).astype(
                jnp.bfloat16
            )
            return running + jnp.einsum(
                "hqk,hkd->hqd", weights, v_block, preferred_element_type=jnp.float32
            )

        running = lax.fori_loop(0, i + 1, attend_inner, jnp.zeros((heads, width, dim), jnp.float32))
        return lax.dynamic_update_slice_in_dim(output, running.astype(jnp.bfloat16), i * width, 1)

    return lax.fori_loop(0, blocks, attend_outer, jnp.zeros((heads, length, dim), jnp.bfloat16))


def value_grads(queries, keys, d_out, peak, total, width, scale):
    heads, length, dim = queries.shape
    blocks = length // width

    def value_outer(j, output):
        j = jnp.asarray(j).astype(jnp.int32)
        k_block = lax.dynamic_slice_in_dim(keys, j * width, width, 1)

        def value_inner(i, running):
            i = jnp.asarray(i).astype(jnp.int32)
            q_block = lax.dynamic_slice_in_dim(queries, i * width, width, 1)
            d_block = lax.dynamic_slice_in_dim(d_out, i * width, width, 1)
            peak_block = lax.dynamic_slice_in_dim(peak, i * width, width, 1)
            total_block = lax.dynamic_slice_in_dim(total, i * width, width, 1)
            scores = block_scores(q_block, k_block, i * width, j * width, scale)
            weights = (jnp.exp(scores - peak_block[:, :, None]) / total_block[:, :, None]).astype(
                jnp.bfloat16
            )
            return running + jnp.einsum(
                "hqk,hqd->hkd", weights, d_block, preferred_element_type=jnp.float32
            )

        running = lax.fori_loop(j, blocks, value_inner, jnp.zeros((heads, width, dim), jnp.float32))
        return lax.dynamic_update_slice_in_dim(output, running.astype(jnp.bfloat16), j * width, 1)

    return lax.fori_loop(0, blocks, value_outer, jnp.zeros((heads, length, dim), jnp.bfloat16))


def local(queries, keys, hidden, value_weight, readout, base_logits, labels, hessian):
    seq_count = lax.axis_size("seq")
    data_count = lax.axis_size("dp")
    token_rows = queries.shape[1]
    heads = queries.shape[2] // HD
    kv_heads = keys.shape[2] // HD
    kv_width = keys.shape[2]
    group = heads // kv_heads
    local_heads = heads // seq_count
    spread_factor = max(1, group // local_heads)
    local_kv = kv_heads * spread_factor // seq_count
    length = token_rows * seq_count
    width = min(512, length)
    scale = 1.0 / math.sqrt(HD)
    columns = lax.all_to_all(hidden, "dp", split_axis=2, concat_axis=0, tiled=True)
    values = sum_at_owner(
        jnp.einsum("std,dk->stk", columns, value_weight, preferred_element_type=jnp.float32).astype(
            jnp.bfloat16
        ),
        "dp",
        0,
    )
    values = values.astype(jnp.bfloat16)

    def widen(array):
        split = array.reshape(1, token_rows, kv_heads, 1, HD)
        split = jnp.broadcast_to(split, (1, token_rows, kv_heads, spread_factor, HD))
        return split.reshape(1, token_rows, seq_count, local_kv * HD)

    paired = jnp.concatenate((widen(keys), widen(values)), axis=3)
    paired = paired.reshape(1, token_rows, seq_count * 2 * local_kv * HD)
    head_queries, head_pairs = (
        several_exchanges(queries, "seq", 2, 2, 1),
        several_exchanges(paired, "seq", 2, 2, 1),
    )

    def heads_first(array, count):
        return array[0].reshape(length, count, HD).transpose(1, 0, 2)

    q_local = heads_first(head_queries, local_heads)
    pair_local = head_pairs[0].reshape(length, 2, local_kv, HD)
    k_local = jnp.repeat(pair_local[:, 0].transpose(1, 0, 2), local_heads // local_kv, axis=0)
    v_local = jnp.repeat(pair_local[:, 1].transpose(1, 0, 2), local_heads // local_kv, axis=0)
    peak, total = row_statistics(q_local, k_local, width, scale)
    attended = attend(q_local, k_local, v_local, peak, total, width, scale)
    attended = attended.transpose(1, 0, 2).reshape(1, length, local_heads * HD)
    mixed = several_exchanges(attended, "seq", 2, 1, 2)
    logits = base_logits[0] + jnp.dot(mixed[0], readout, preferred_element_type=jnp.float32)
    softmax_rows = jax.nn.softmax(logits, axis=1)
    chosen = labels[0][:, None] == lax.broadcasted_iota(jnp.int32, logits.shape, 1)
    d_logits = (softmax_rows - chosen.astype(jnp.float32)).astype(jnp.bfloat16)
    d_mixed = jnp.einsum("tc,ec->te", d_logits, readout, preferred_element_type=jnp.float32).astype(
        jnp.bfloat16
    )
    d_heads = several_exchanges(d_mixed[None], "seq", 2, 2, 1)
    d_local = heads_first(d_heads, local_heads)
    d_head = value_grads(q_local, k_local, d_local, peak, total, width, scale)
    d_head = d_head.transpose(1, 0, 2).reshape(1, length, local_heads * HD)
    d_tokens = lax.all_to_all(d_head, "seq", split_axis=1, concat_axis=2, tiled=True)
    d_values = d_tokens[0].astype(jnp.float32).reshape(token_rows, kv_heads, group, HD).sum(axis=2)
    d_values = d_values.reshape(1, token_rows, kv_width).astype(jnp.bfloat16)
    partial_value = jnp.einsum(
        "stk,std->kd", collect(d_values, "dp", 0), columns, preferred_element_type=jnp.float32
    )
    grad_sum = sum_at_owner(partial_value.astype(jnp.bfloat16), "seq", 0)
    tokens_all = length * data_count
    estimate = grad_sum * grad_sum / tokens_all
    return (estimate, beta_two * hessian + (1.0 - beta_two) * estimate)


def solution(mesh):
    placed = (
        P("dp", "seq", None),
        P("dp", "seq", None),
        P("dp", "seq", None),
        P("dp", None),
        P(),
        P("dp", "seq", None),
        P("dp", "seq"),
        P("seq", "dp"),
    )
    return jax.shard_map(
        local,
        mesh=mesh,
        in_specs=placed,
        out_specs=(P("seq", "dp"), P("seq", "dp")),
        check_vma=False,
    )
```

profile of v0, /device:TPU:1, one launch (start us, length us, event | category | flops | bytes accessed | tf_op | source)
XLA Modules:
  0.0 689.4 jit_solution(15799862219191184211)
XLA Ops:
  0.6 5.7 copy.51
  6.8 23.3 %reduce.11 = bf16[4096,128]{1,0:T(8,128)(2,1)S(1)} reduce(bf16[4096,1,128]{2,1,0:T(2,128)(2,1)} %bitcast.184, bf16[]{:T(256)} %broadcast.149), dimensions={1}, to_apply=%bitcast.130.reduce_sub_computation | reduce | bytes 2097154
  31.3 7.3 %all-to-all-start = ((bf16[8,2,32768]{2,1,0:T(2,128)(2,1)}), bf16[8,2,32768]{2,1,0:T(2,128)(2,1)}, u32[]{:S(2)}, u32[]{:S(2)}) async-start(bf16[8,2,32768]{2,1,0:T(2,128)(2,1)} %reshape.161), calls=%async_computation | async-start | bytes 2097152 | tf_op jit(solution)/shard_map/all_to_all | solution.py:170
  44.3 9.4 %all-to-all-done = bf16[8,2,32768]{2,1,0:T(2,128)(2,1)} async-done(((bf16[8,2,32768]{2,1,0:T(2,128)(2,1)}), bf16[8,2,32768]{2,1,0:T(2,128)(2,1)}, u32[]{:S(2)}, u32[]{:S(2)}) %all-to-all-start) | async-done | bytes 1048608 | tf_op jit(solution)/shard_map/all_to_all | solution.py:170
  53.7 9.8 %all-to-all-start.4 = ((bf16[32,1,64,128]{3,2,1,0:T(8,128)(2,1)}), bf16[32,1,64,128]{3,2,1,0:T(8,128)(2,1)}, u32[]{:S(2)}, u32[]{:S(2)}) async-start(bf16[32,1,64,128]{3,2,1,0:T(8,128)(2,1)} %copy.59), calls=%async_computation.4 | async-start | bytes 1048576 | tf_op jit(solution)/shard_map/all_to_all | solution.py:45
  63.5 5.8 reshape.162
  78.8 7.6 %all-to-all-start.1 = ((bf16[8,1,128,1024]{3,2,1,0:T(8,128)(2,1)}), bf16[8,1,128,1024]{3,2,1,0:T(8,128)(2,1)}, u32[]{:S(2)}, u32[]{:S(2)}) async-start(bf16[8,1,128,1024]{3,2,1,0:T(8,128)(2,1)} %convert_bitcast_fusion), calls=%async_computation.1 | async-start | bytes 4194304 | tf_op jit(solution)/shard_map/all_to_all | solution.py:22
  87.5 25.2 %all-to-all-done.1 = bf16[8,1,128,1024]{3,2,1,0:T(8,128)(2,1)} async-done(((bf16[8,1,128,1024]{3,2,1,0:T(8,128)(2,1)}), bf16[8,1,128,1024]{3,2,1,0:T(8,128)(2,1)}, u32[]{:S(2)}, u32[]{:S(2)}) %all-to-all-start.1) | async-done | bytes 2097184 | tf_op jit(solution)/shard_map/all_to_all | solution.py:22
  112.7 5.2 all-to-all-start.5
  122.2 11.1 %all-to-all-done.5 = bf16[32,1,64,128]{3,2,1,0:T(8,128)(2,1)} async-done(((bf16[32,1,64,128]{3,2,1,0:T(8,128)(2,1)}), bf16[32,1,64,128]{3,2,1,0:T(8,128)(2,1)}, u32[]{:S(2)}, u32[]{:S(2)}) %all-to-all-start.5) | async-done | bytes 524320 | tf_op jit(solution)/shard_map/all_to_all | solution.py:45
  133.3 31.7 %all_to_all.82 = bf16[32,1,64,256]{3,2,1,0:T(8,128)(2,1)} all-to-all(bf16[32,1,64,256]{3,2,1,0:T(8,128)(2,1)S(1)} %get-tuple-element.816), channel_id=1, replica_groups=mesh['seq'=32,'dp'=8] {'seq'}, dimensions={0} | all-to-all | bytes 2097152 | tf_op jit(solution)/shard_map/all_to_all | solution.py:45
  165.0 7.0 %all-to-all-start.3 = ((bf16[32,1,64,256]{3,2,1,0:T(8,128)(2,1)}), bf16[32,1,64,256]{3,2,1,0:T(8,128)(2,1)}, u32[]{:S(2)}, u32[]{:S(2)}) async-start(bf16[32,1,64,256]{3,2,1,0:T(8,128)(2,1)} %get-tuple-element.817), calls=%async_computation.3 | async-start | bytes 2097152 | tf_op jit(solution)/shard_map/all_to_all | solution.py:45
  173.3 23.8 %all-to-all-done.3 = bf16[32,1,64,256]{3,2,1,0:T(8,128)(2,1)} async-done(((bf16[32,1,64,256]{3,2,1,0:T(8,128)(2,1)}), bf16[32,1,64,256]{3,2,1,0:T(8,128)(2,1)}, u32[]{:S(2)}, u32[]{:S(2)}) %all-to-all-start.3) | async-done | bytes 1048608 | tf_op jit(solution)/shard_map/all_to_all | solution.py:45
  204.2 6.8 fusion.74
  211.0 5.4 copy.75
  219.9 59.3 %while.120 = (s32[]{:T(128)}, f32[1,4096]{1,0:T(1,128)}, f32[1,4096]{1,0:T(1,128)}, bf16[1,4096,128]{2,1,0:T(8,128)(2,1)S(1)}, bf16[1,4096,128]{2,1,0:T(8,128)(2...) while((s32[]{:T(128)}, f32[1,4096]{1,0:T(1,128)}, ...), condition=%wide.region_6.7_spmd, body=%wide.region_1.6_spmd.sunk | while | flops 68683792 | bytes 2669010 | solution.py:97
  225.7 4.5 while.125
  230.9 6.0 while.125
  237.6 7.5 %while.125 = (s32[]{:T(128)}, f32[1,512]{1,0:T(1,128)S(1)}, f32[1,512]{1,0:T(1,128)S(1)}, s32[]{:T(128)}, s32[]{:T(128)}, /*index=5*/bf16[1,4096,128]{2,1,0:T(8,...) while((s32[]{:T(128)}, f32[1,512]{1,0:T(1,128)S(1)}, ...), condition=%wide.region_5.5_spmd, body=%wide.region_2.4_spmd.sunk | while | flops 68683784 | bytes 2394279 | solution.py:91
  245.7 9.0 %while.125 = (s32[]{:T(128)}, f32[1,512]{1,0:T(1,128)S(1)}, f32[1,512]{1,0:T(1,128)S(1)}, s32[]{:T(128)}, s32[]{:T(128)}, /*index=5*/bf16[1,4096,128]{2,1,0:T(8,...) while((s32[]{:T(128)}, f32[1,512]{1,0:T(1,128)S(1)}, ...), condition=%wide.region_5.5_spmd, body=%wide.region_2.4_spmd.sunk | while | flops 68683784 | bytes 2394279 | solution.py:91
  255.4 10.5 %while.125 = (s32[]{:T(128)}, f32[1,512]{1,0:T(1,128)S(1)}, f32[1,512]{1,0:T(1,128)S(1)}, s32[]{:T(128)}, s32[]{:T(128)}, /*index=5*/bf16[1,4096,128]{2,1,0:T(8,...) while((s32[]{:T(128)}, f32[1,512]{1,0:T(1,128)S(1)}, ...), condition=%wide.region_5.5_spmd, body=%wide.region_2.4_spmd.sunk | while | flops 68683784 | bytes 2394279 | solution.py:91
  266.6 12.1 %while.125 = (s32[]{:T(128)}, f32[1,512]{1,0:T(1,128)S(1)}, f32[1,512]{1,0:T(1,128)S(1)}, s32[]{:T(128)}, s32[]{:T(128)}, /*index=5*/bf16[1,4096,128]{2,1,0:T(8,...) while((s32[]{:T(128)}, f32[1,512]{1,0:T(1,128)S(1)}, ...), condition=%wide.region_5.5_spmd, body=%wide.region_2.4_spmd.sunk | while | flops 68683784 | bytes 2394279 | solution.py:91
  279.3 5.4 copy.76
  288.1 74.3 %while.122 = (s32[]{:T(128)}, bf16[1,4096,128]{2,1,0:T(8,128)(2,1)}, bf16[1,4096,128]{2,1,0:T(8,128)(2,1)S(1)}, f32[1,4096]{1,0:T(1,128)}, f32[1,4096]{1,0:T(1,1...) while((s32[]{:T(128)}, bf16[1,4096,128]{2,1,0:T(8,128)(2,1)}, ...), condition=%wide.region_10.11_spmd, body=%wide.region_7.10_spmd.sunk | while | flops 135922688 | bytes 1857014 | solution.py:125
  296.9 5.2 while.126
  303.6 7.0 %while.126 = (s32[]{:T(128)}, f32[1,512,128]{2,1,0:T(8,128)S(1)}, s32[]{:T(128)}, s32[]{:T(128)}, bf16[1,4096,128]{2,1,0:T(8,128)(2,1)}, /*index=5*/bf16[1,512,1...) while((s32[]{:T(128)}, f32[1,512,128]{2,1,0:T(8,128)S(1)}, ...), condition=%wide.region_9.9_spmd, body=%wide.region_8.8_spmd.sunk | while | flops 135857152 | bytes 930995 | solution.py:122
  312.0 8.7 %while.126 = (s32[]{:T(128)}, f32[1,512,128]{2,1,0:T(8,128)S(1)}, s32[]{:T(128)}, s32[]{:T(128)}, bf16[1,4096,128]{2,1,0:T(8,128)(2,1)}, /*index=5*/bf16[1,512,1...) while((s32[]{:T(128)}, f32[1,512,128]{2,1,0:T(8,128)S(1)}, ...), condition=%wide.region_9.9_spmd, body=%wide.region_8.8_spmd.sunk | while | flops 135857152 | bytes 930995 | solution.py:122
  322.1 10.5 %while.126 = (s32[]{:T(128)}, f32[1,512,128]{2,1,0:T(8,128)S(1)}, s32[]{:T(128)}, s32[]{:T(128)}, bf16[1,4096,128]{2,1,0:T(8,128)(2,1)}, /*index=5*/bf16[1,512,1...) while((s32[]{:T(128)}, f32[1,512,128]{2,1,0:T(8,128)S(1)}, ...), condition=%wide.region_9.9_spmd, body=%wide.region_8.8_spmd.sunk | while | flops 135857152 | bytes 930995 | solution.py:122
  334.1 12.2 %while.126 = (s32[]{:T(128)}, f32[1,512,128]{2,1,0:T(8,128)S(1)}, s32[]{:T(128)}, s32[]{:T(128)}, bf16[1,4096,128]{2,1,0:T(8,128)(2,1)}, /*index=5*/bf16[1,512,1...) while((s32[]{:T(128)}, f32[1,512,128]{2,1,0:T(8,128)S(1)}, ...), condition=%wide.region_9.9_spmd, body=%wide.region_8.8_spmd.sunk | while | flops 135857152 | bytes 930995 | solution.py:122
  347.7 14.0 %while.126 = (s32[]{:T(128)}, f32[1,512,128]{2,1,0:T(8,128)S(1)}, s32[]{:T(128)}, s32[]{:T(128)}, bf16[1,4096,128]{2,1,0:T(8,128)(2,1)}, /*index=5*/bf16[1,512,1...) while((s32[]{:T(128)}, f32[1,512,128]{2,1,0:T(8,128)S(1)}, ...), condition=%wide.region_9.9_spmd, body=%wide.region_8.8_spmd.sunk | while | flops 135857152 | bytes 930995 | solution.py:122
  364.5 21.2 %all_to_all.83 = bf16[32,1,64,128]{3,2,1,0:T(8,128)(2,1)} all-to-all(bf16[32,1,64,128]{3,2,1,0:T(8,128)(2,1)S(1)} %get-tuple-element.820), channel_id=1, replica_groups=mesh['seq'=32,'dp'=8] {'seq'}, dimensions={0} | all-to-all | bytes 1048576 | tf_op jit(solution)/shard_map/all_to_all | solution.py:45
  385.6 6.3 all-to-all-start.7
  394.4 11.9 %all-to-all-done.7 = bf16[32,1,64,128]{3,2,1,0:T(8,128)(2,1)} async-done(((bf16[32,1,64,128]{3,2,1,0:T(8,128)(2,1)}), bf16[32,1,64,128]{3,2,1,0:T(8,128)(2,1)}, u32[]{:S(2)}, u32[]{:S(2)}) %all-to-all-start.7) | async-done | bytes 524320 | tf_op jit(solution)/shard_map/all_to_all | solution.py:45
  414.0 19.9 %all_to_all.84 = bf16[32,1,64,128]{3,2,1,0:T(8,128)(2,1)} all-to-all(bf16[32,1,64,128]{3,2,1,0:T(8,128)(2,1)S(1)} %get-tuple-element.818), channel_id=1, replica_groups=mesh['seq'=32,'dp'=8] {'seq'}, dimensions={0} | all-to-all | bytes 1048576 | tf_op jit(solution)/shard_map/all_to_all | solution.py:45
  433.9 6.1 all-to-all-start.9
  440.0 13.0 %all-to-all-done.9 = bf16[32,1,64,128]{3,2,1,0:T(8,128)(2,1)} async-done(((bf16[32,1,64,128]{3,2,1,0:T(8,128)(2,1)}), bf16[32,1,64,128]{3,2,1,0:T(8,128)(2,1)}, u32[]{:S(2)}, u32[]{:S(2)}) %all-to-all-start.9) | async-done | bytes 524320 | tf_op jit(solution)/shard_map/all_to_all | solution.py:45
  456.4 99.4 %while.124 = (s32[]{:T(128)}, bf16[1,4096,128]{2,1,0:T(8,128)(2,1)}, bf16[1,4096,128]{2,1,0:T(8,128)(2,1)}, bf16[1,4096,128]{2,1,0:T(8,128)(2,1)S(1)}, f32[1,409...) while((s32[]{:T(128)}, bf16[1,4096,128]{2,1,0:T(8,128)(2,1)}, ...), condition=%wide.region_16.17_spmd, body=%wide.region_13.16_spmd.sunk | while | flops 135922688 | bytes 1856998 | solution.py:153
  457.3 19.2 %while.127 = (s32[]{:T(128)}, f32[1,512,128]{2,1,0:T(8,128)S(1)}, s32[]{:T(128)}, bf16[1,4096,128]{2,1,0:T(8,128)(2,1)S(1)}, bf16[1,512,128]{2,1,0:T(8,128)(2,1)...) while((s32[]{:T(128)}, f32[1,512,128]{2,1,0:T(8,128)S(1)}, ...), condition=%wide.region_15.15_spmd, body=%wide.region_14.14_spmd.sunk | while | flops 135857152 | bytes 939183 | solution.py:150
  478.2 16.8 %while.127 = (s32[]{:T(128)}, f32[1,512,128]{2,1,0:T(8,128)S(1)}, s32[]{:T(128)}, bf16[1,4096,128]{2,1,0:T(8,128)(2,1)S(1)}, bf16[1,512,128]{2,1,0:T(8,128)(2,1)...) while((s32[]{:T(128)}, f32[1,512,128]{2,1,0:T(8,128)S(1)}, ...), condition=%wide.region_15.15_spmd, body=%wide.region_14.14_spmd.sunk | while | flops 135857152 | bytes 939183 | solution.py:150
  496.6 14.4 %while.127 = (s32[]{:T(128)}, f32[1,512,128]{2,1,0:T(8,128)S(1)}, s32[]{:T(128)}, bf16[1,4096,128]{2,1,0:T(8,128)(2,1)S(1)}, bf16[1,512,128]{2,1,0:T(8,128)(2,1)...) while((s32[]{:T(128)}, f32[1,512,128]{2,1,0:T(8,128)S(1)}, ...), condition=%wide.region_15.15_spmd, body=%wide.region_14.14_spmd.sunk | while | flops 135857152 | bytes 939183 | solution.py:150
  512.6 12.0 %while.127 = (s32[]{:T(128)}, f32[1,512,128]{2,1,0:T(8,128)S(1)}, s32[]{:T(128)}, bf16[1,4096,128]{2,1,0:T(8,128)(2,1)S(1)}, bf16[1,512,128]{2,1,0:T(8,128)(2,1)...) while((s32[]{:T(128)}, f32[1,512,128]{2,1,0:T(8,128)S(1)}, ...), condition=%wide.region_15.15_spmd, body=%wide.region_14.14_spmd.sunk | while | flops 135857152 | bytes 939183 | solution.py:150
  526.2 9.6 %while.127 = (s32[]{:T(128)}, f32[1,512,128]{2,1,0:T(8,128)S(1)}, s32[]{:T(128)}, bf16[1,4096,128]{2,1,0:T(8,128)(2,1)S(1)}, bf16[1,512,128]{2,1,0:T(8,128)(2,1)...) while((s32[]{:T(128)}, f32[1,512,128]{2,1,0:T(8,128)S(1)}, ...), condition=%wide.region_15.15_spmd, body=%wide.region_14.14_spmd.sunk | while | flops 135857152 | bytes 939183 | solution.py:150
  537.4 7.2 %while.127 = (s32[]{:T(128)}, f32[1,512,128]{2,1,0:T(8,128)S(1)}, s32[]{:T(128)}, bf16[1,4096,128]{2,1,0:T(8,128)(2,1)S(1)}, bf16[1,512,128]{2,1,0:T(8,128)(2,1)...) while((s32[]{:T(128)}, f32[1,512,128]{2,1,0:T(8,128)S(1)}, ...), condition=%wide.region_15.15_spmd, body=%wide.region_14.14_spmd.sunk | while | flops 135857152 | bytes 939183 | solution.py:150
  546.3 4.8 while.127
  560.1 23.3 %reduce.12 = bf16[4096,128]{1,0:T(8,128)(2,1)S(1)} reduce(bf16[4096,1,128]{2,1,0:T(2,128)(2,1)} %bitcast.185, bf16[]{:T(256)} %broadcast.149), dimensions={1}, to_apply=%bitcast.143.reduce_sub_computation | reduce | bytes 2097154
  584.6 30.0 %all_to_all.87 = bf16[32,2,8192]{2,1,0:T(2,128)(2,1)S(1)} all-to-all(bf16[32,2,8192]{2,1,0:T(2,128)(2,1)} %reshape.163), channel_id=1, replica_groups=mesh['seq'=32,'dp'=8] {'seq'}, dimensions={0} | all-to-all | bytes 2097152 | tf_op jit(solution)/shard_map/all_to_all | solution.py:214
  620.4 35.7 %all_to_all.85 = bf16[8,1,128,1024]{2,3,1,0:T(8,128)(2,1)S(1)} all-to-all(bf16[8,1,128,1024]{2,3,1,0:T(8,128)(2,1)S(1)} %broadcast_in_dim.44), channel_id=1, replica_groups=mesh['seq'=32,'dp'=8] {'dp'}, dimensions={0} | all-to-all | bytes 4194304 | tf_op jit(solution)/shard_map/all_to_all | solution.py:51
  657.4 31.2 %all_to_all.86 = bf16[32,32,512]{2,1,0:T(8,128)(2,1)S(1)} all-to-all(bf16[32,32,512]{2,1,0:T(8,128)(2,1)S(1)} %bitcast.203), channel_id=1, replica_groups=mesh['seq'=32,'dp'=8] {'seq'}, dimensions={0} | all-to-all | bytes 2097152 | tf_op jit(solution)/shard_map/all_to_all | solution.py:22
  (552 shorter events, 306.6 us)
Async XLA Ops:
  0.6 410.1 %copy-start = (bf16[4096,256]{1,0:T(8,128)(2,1)S(1)}, bf16[4096,256]{1,0:T(8,128)(2,1)}, u32[]{:S(2)}) copy-start(bf16[4096,256]{1,0:T(8,128)(2,1)} %param.24) | copy-start | bytes 6291460
  31.3 22.4 %all-to-all-start = ((bf16[8,2,32768]{2,1,0:T(2,128)(2,1)}), bf16[8,2,32768]{2,1,0:T(2,128)(2,1)}, u32[]{:S(2)}, u32[]{:S(2)}) async-start(bf16[8,2,32768]{2,1,0:T(2,128)(2,1)} %reshape.161), calls=%async_computation | async-start | bytes 2097152 | tf_op jit(solution)/shard_map/all_to_all | solution.py:170
  53.7 25.1 %all-to-all-start.4 = ((bf16[32,1,64,128]{3,2,1,0:T(8,128)(2,1)}), bf16[32,1,64,128]{3,2,1,0:T(8,128)(2,1)}, u32[]{:S(2)}, u32[]{:S(2)}) async-start(bf16[32,1,64,128]{3,2,1,0:T(8,128)(2,1)} %copy.59), calls=%async_computation.4 | async-start | bytes 1048576 | tf_op jit(solution)/shard_map/all_to_all | solution.py:45
  76.4 9.9 %copy-start.1 = (bf16[32,1,64,128]{2,3,0,1:T(8,128)(2,1)S(1)}, bf16[32,1,64,128]{2,3,0,1:T(8,128)(2,1)}, u32[]{:S(2)}) copy-start(bf16[32,1,64,128]{2,3,0,1:T(8,128)(2,1)} %get-tuple-element.823) | copy-start | bytes 1572868
  78.8 33.9 %all-to-all-start.1 = ((bf16[8,1,128,1024]{3,2,1,0:T(8,128)(2,1)}), bf16[8,1,128,1024]{3,2,1,0:T(8,128)(2,1)}, u32[]{:S(2)}, u32[]{:S(2)}) async-start(bf16[8,1,128,1024]{3,2,1,0:T(8,128)(2,1)} %convert_bitcast_fusion), calls=%async_computation.1 | async-start | bytes 4194304 | tf_op jit(solution)/shard_map/all_to_all | solution.py:22
  86.4 31.6 %copy-start.3 = (bf16[1,128,1024]{2,1,0:T(8,128)(2,1)S(1)}, bf16[1,128,1024]{2,1,0:T(8,128)(2,1)}, u32[]{:S(2)}) copy-start(bf16[1,128,1024]{2,1,0:T(8,128)(2,1)} %param.21) | copy-start | bytes 786436
  112.7 20.6 %all-to-all-start.5 = ((bf16[32,1,64,128]{3,2,1,0:T(8,128)(2,1)}), bf16[32,1,64,128]{3,2,1,0:T(8,128)(2,1)}, u32[]{:S(2)}, u32[]{:S(2)}) async-start(bf16[32,1,64,128]{3,2,1,0:T(8,128)(2,1)} %copy.60), calls=%async_computation.5 | async-start | bytes 1048576 | tf_op jit(solution)/shard_map/all_to_all | solution.py:45
  165.0 32.1 %all-to-all-start.3 = ((bf16[32,1,64,256]{3,2,1,0:T(8,128)(2,1)}), bf16[32,1,64,256]{3,2,1,0:T(8,128)(2,1)}, u32[]{:S(2)}, u32[]{:S(2)}) async-start(bf16[32,1,64,256]{3,2,1,0:T(8,128)(2,1)} %get-tuple-element.817), calls=%async_computation.3 | async-start | bytes 2097152 | tf_op jit(solution)/shard_map/all_to_all | solution.py:45
  385.6 20.6 %all-to-all-start.7 = ((bf16[32,1,64,128]{3,2,1,0:T(8,128)(2,1)}), bf16[32,1,64,128]{3,2,1,0:T(8,128)(2,1)}, u32[]{:S(2)}, u32[]{:S(2)}) async-start(bf16[32,1,64,128]{3,2,1,0:T(8,128)(2,1)} %get-tuple-element.821), calls=%async_computation.7 | async-start | bytes 1048576 | tf_op jit(solution)/shard_map/all_to_all | solution.py:45
  394.4 16.4 %copy-start.4 = (f32[1,128,256]{2,1,0:T(8,128)S(1)}, f32[1,128,256]{2,1,0:T(8,128)}, u32[]{:S(2)}) copy-start(f32[1,128,256]{2,1,0:T(8,128)} %param.25) | copy-start | bytes 393220
  410.8 0.8 copy-start.6
  433.9 19.1 %all-to-all-start.9 = ((bf16[32,1,64,128]{3,2,1,0:T(8,128)(2,1)}), bf16[32,1,64,128]{3,2,1,0:T(8,128)(2,1)}, u32[]{:S(2)}, u32[]{:S(2)}) async-start(bf16[32,1,64,128]{3,2,1,0:T(8,128)(2,1)} %get-tuple-element.819), calls=%async_computation.9 | async-start | bytes 1048576 | tf_op jit(solution)/shard_map/all_to_all | solution.py:45
  620.4 35.7 %copy-start.2 = (bf16[1,128,8,512]{3,1,2,0:T(8,128)(2,1)S(1)}, bf16[1,128,8,512]{3,1,2,0:T(8,128)(2,1)}, u32[]{:S(2)}) copy-start(bf16[1,128,8,512]{3,1,2,0:T(8,128)(2,1)} %copy.52) | copy-start | bytes 3145732
  657.4 31.4 %copy-start.5 = (f32[32,512]{1,0:T(8,128)S(1)}, f32[32,512]{1,0:T(8,128)}, u32[]{:S(2)}) copy-start(f32[32,512]{1,0:T(8,128)} %param.27) | copy-start | bytes 196612
where the time goes:
time: 697 us; the launch traced here: 689 us
  matrix products  172 us (25%)
  blocking collectives  170 us (24%)
  local copies, waits for them, and re-layouts  118 us (17%)
  waiting for transfers between devices  96.7 us (14%)
  other arithmetic  78 us (11%)
  starting transfers between devices  49.3 us (7%)
    all_to_all x3, blocking collectives, several_exchanges(): lax.all_to_all(share, axis, split_axis=0, concat_axis=0, tiled=True)  72.8 us
    all_to_all x5, waiting for transfers between devices, several_exchanges(): lax.all_to_all(share, axis, split_axis=0, concat_axis=0, tiled=True)  62.1 us
    dot_general x36, matrix products, attend_inner(): jnp.einsum('hqk,hkd->hqd', weights, v_block, preferred_element_type=jnp.f...  61.3 us
    dot_general x36, matrix products, value_inner(): jnp.einsum('hqk,hqd->hkd', weights, d_block, preferred_element_type=jnp.f...  59.8 us
    unnamed x2, other arithmetic  46.7 us
    dot_general x36, matrix products, block_scores(): jnp.einsum('hqd,hkd->hqk', q_block, k_block, preferred_element_type=jnp.f...  44.3 us
    all_to_all x1, blocking collectives, sent_to_all(): return lax.all_to_all(copies, axis, split_axis=0, concat_axis=0, tiled=True)  35.7 us
    all_to_all x5, starting transfers between devices, several_exchanges(): lax.all_to_all(share, axis, split_axis=0, concat_axis=0, tiled=True)  34.4 us
  transfers between devices with their start and end apart: 7, of which 7 were waited for; matrix products, arithmetic and copies ran while one was open for 4% of the time, Pallas kernels for 0%

commit v1 on v0

v1 whole, which is shorter than its diff:
```python
import functools
import math
import types

import jax
import jax.numpy as jnp
from jax import lax
from jax.experimental import pallas as pl
from jax.experimental.pallas import tpu as pltpu
from jax.sharding import PartitionSpec as P

HD = 128
TOK = 128
SMALL = -1.0e30
beta_two = 0.99
MESH = pl.DeviceIdType.MESH
F32 = jnp.float32
BF16 = jnp.bfloat16
VMEM = pl.BlockSpec(memory_space=pltpu.VMEM)
ANY = pl.BlockSpec(memory_space=pl.ANY)


def sizes_of(seq, dp):
    n = types.SimpleNamespace(S=seq, P=dp, C=2, X=dp // 2)
    n.Y = 4 if seq == 32 else 2
    n.Z = seq // n.Y
    return n


def place():
    return lax.axis_index("seq"), lax.axis_index("dp")


def rem(a, b):
    return lax.rem(a, jnp.int32(b))


def loop(low, high, step):
    def body(i, carry):
        step(i)
        return carry

    lax.fori_loop(low, high, body, 0)


def aligned(start, size):
    return pl.ds(pl.multiple_of(start, size), size)


def send(src, dst, send_sem, recv_sem, seq, dp):
    return pltpu.make_async_remote_copy(
        src_ref=src,
        dst_ref=dst,
        send_sem=send_sem,
        recv_sem=recv_sem,
        device_id=(seq, dp),
        device_id_type=MESH,
    )


def greet(peers):
    barrier = pltpu.get_barrier_semaphore()
    count = 0
    for low, high, where in peers:

        def one(d, where=where):
            seq, dp = where(d)
            pl.semaphore_signal(barrier, inc=1, device_id=(seq, dp), device_id_type=MESH)

        loop(low, high, one)
        count += high - low
    pl.semaphore_wait(barrier, count)


def front_kernel(
    n,
    hidden,
    queries,
    keys,
    weight,
    cols,
    qz,
    kz,
    vz,
    part,
    pair,
    both,
    xin,
    val,
    loc,
    hs,
    hr,
    qs,
    qr,
    ks,
    kr,
    kys,
    kyr,
    cs,
    cr,
    xs,
    xr,
    vs,
    vr,
    vys,
    vyr,
):
    seq, dp = place()
    Z, Y, X, C, PP = n.Z, n.Y, n.X, n.C, n.P
    z, y = seq // Y, rem(seq, Y)
    x, c = dp // C, rem(dp, C)
    feat = hidden.shape[1] // PP
    qw = queries.shape[1] // Z

    def zpeer(d):
        return rem(z + d, Z) * Y + y, dp

    def ypeer(e):
        return z * Y + rem(y + e, Y), dp

    def ppeer(d):
        return seq, rem(dp + d, PP)

    greet(((1, Z, zpeer), (1, Y, ypeer), (1, PP, ppeer)))

    def slot_of(p):
        return rem(p, C) * X + p // C

    def lanes(ref, i, width):
        return ref.at[:, aligned(i * width, width)]

    def k_send(d):
        to = rem(z + d, Z)
        return send(lanes(keys, to, HD), kz.at[seq], ks.at[d], kr.at[d], to * Y + y, dp)

    def h_send(d):
        to = rem(dp + d, PP)
        return send(lanes(hidden, to, feat), cols.at[slot_of(dp)], hs.at[d], hr.at[d], seq, to)

    def q_send(d):
        to = rem(z + d, Z)
        return send(lanes(queries, to, qw), qz.at[z], qs.at[d], qr.at[d], to * Y + y, dp)

    loop(1, Z, lambda d: k_send(d).start())
    loop(1, PP, lambda d: h_send(d).start())
    loop(1, Z, lambda d: q_send(d).start())
    own_k = pltpu.make_async_copy(lanes(keys, z, HD), kz.at[seq], loc.at[0])
    own_h = pltpu.make_async_copy(lanes(hidden, dp, feat), cols.at[slot_of(dp)], loc.at[1])
    own_q = pltpu.make_async_copy(lanes(queries, z, qw), qz.at[z], loc.at[2])
    own_k.start()
    own_h.start()
    own_q.start()

    def forward(ref, first, d, e, ssem, rsem):
        at = rem(z - d + Z, Z) * Y + y
        src = first if first is not None else ref.at[at]
        to = rem(y + e, Y)
        return send(src, ref.at[at], ssem.at[d, e], rsem.at[d, e], z * Y + to, dp)

    def forward_all(ref, mine, sent, ssem, rsem):
        loop(1, Y, lambda e: forward(ref, mine, 0, e, ssem, rsem).start())

        def step(d):
            sent(d).wait_recv()
            loop(1, Y, lambda e: forward(ref, None, d, e, ssem, rsem).start())

        loop(1, Z, step)

    def forward_done(ref, mine, ssem, rsem):
        loop(1, Y, lambda e: forward(ref, mine, 0, e, ssem, rsem).wait())
        loop(1, Z, lambda d: loop(1, Y, lambda e: forward(ref, None, d, e, ssem, rsem).wait()))

    forward_all(kz, lanes(keys, z, HD), k_send, kys, kyr)

    own_h.wait()
    loop(1, PP, lambda d: h_send(d).wait_recv())
    rows = X * TOK
    width = min(512, part.shape[1])

    def product(half):
        block = cols[pl.ds(half * X, X)].reshape(rows, feat)
        for w in range(0, part.shape[1], width):
            part[pl.ds(pl.multiple_of(half * rows, rows), rows), w : w + width] = jnp.dot(
                block, weight[:, w : w + width], preferred_element_type=F32
            ).astype(BF16)

    other = 1 - c

    def c_send(i):
        row = aligned((other * X + i) * TOK, TOK)
        return send(part.at[row], pair.at[i], cs.at[i], cr.at[i], seq, x * C + other)

    product(other)
    loop(0, X, lambda i: c_send(i).start())
    product(c)

    def x_send(d):
        to = rem(x + d, X)
        return send(both.at[to], xin.at[d], xs.at[d], xr.at[d], seq, to * C + c)

    def join(d):
        to = rem(x + d, X)
        c_send(to).wait_recv()
        mine = part[aligned((c * X + to) * TOK, TOK)].astype(F32)
        both[to] = (mine + pair[to].astype(F32)).astype(BF16)

    def join_send(d):
        join(d)
        x_send(d).start()

    loop(1, X, join_send)
    join(jnp.int32(X))
    total = both[x].astype(F32)
    for d in range(1, X):
        x_send(d).wait_recv()
        total = total + xin[d].astype(F32)
    val[...] = total.astype(BF16)

    def v_send(d):
        to = rem(z + d, Z)
        return send(lanes(val, to, HD), vz.at[seq], vs.at[d], vr.at[d], to * Y + y, dp)

    own_v = pltpu.make_async_copy(lanes(val, z, HD), vz.at[seq], loc.at[3])
    loop(1, Z, lambda d: v_send(d).start())
    own_v.start()
    forward_all(vz, lanes(val, z, HD), v_send, vys, vyr)

    own_k.wait()
    own_q.wait()
    own_v.wait()
    loop(1, Z, lambda d: q_send(d).wait())
    loop(1, Z, lambda d: k_send(d).wait_send())
    loop(1, Z, lambda d: v_send(d).wait_send())
    loop(1, PP, lambda d: h_send(d).wait_send())
    loop(0, X, lambda i: c_send(i).wait_send())
    loop(1, X, lambda d: x_send(d).wait_send())
    forward_done(kz, lanes(keys, z, HD), kys, kyr)
    forward_done(vz, lanes(val, z, HD), vys, vyr)


def front(n, hidden, queries, keys, weight):
    feat = hidden.shape[1] // n.P
    qw = queries.shape[1] // n.Z
    kv = keys.shape[1]
    dma = pltpu.SemaphoreType.DMA
    shape = jax.ShapeDtypeStruct
    return pl.pallas_call(
        functools.partial(front_kernel, n),
        out_shape=(
            shape((n.P, TOK, feat), BF16),
            shape((n.Z, TOK, qw), BF16),
            shape((n.S, TOK, HD), BF16),
            shape((n.S, TOK, HD), BF16),
        ),
        in_specs=[ANY, ANY, ANY, VMEM],
        out_specs=(VMEM, VMEM, VMEM, VMEM),
        scratch_shapes=[
            pltpu.VMEM((n.P * TOK, kv), BF16),
            pltpu.VMEM((n.X, TOK, kv), BF16),
            pltpu.VMEM((n.X, TOK, kv), BF16),
            pltpu.VMEM((n.X, TOK, kv), BF16),
            pltpu.VMEM((TOK, kv), BF16),
            dma((4,)),
            dma((n.P,)),
            dma((n.P,)),
            dma((n.Z,)),
            dma((n.Z,)),
            dma((n.Z,)),
            dma((n.Z,)),
            dma((n.Z, n.Y)),
            dma((n.Z, n.Y)),
            dma((n.X,)),
            dma((n.X,)),
            dma((n.X,)),
            dma((n.X,)),
            dma((n.Z,)),
            dma((n.Z,)),
            dma((n.Z, n.Y)),
            dma((n.Z, n.Y)),
        ],
        compiler_params=pltpu.CompilerParams(collective_id=0, has_side_effects=True),
        name="front",
    )(hidden, queries, keys, weight)


def contract(a, b, da, db):
    return lax.dot_general(a, b, (((da,), (db,)), ((), ())), preferred_element_type=F32)


def attend_kernel(n, group, qz, k, v, readout, logits, kept, inverse, raw, vt, out):
    y = rem(lax.axis_index("seq"), n.Y)
    chunk = n.Y * TOK
    wide = group * TOK
    factor = math.log2(math.e) / math.sqrt(HD)

    def turn(j):
        vt[j] = v[aligned(j * chunk, chunk), :].astype(F32).T.astype(BF16)

    loop(0, n.Z, turn)

    def fold(a, op):
        return op(a.reshape(chunk // 8, 8, wide), axis=0)

    def block(t):
        q_block = qz[t]
        q_rows = jnp.concatenate([q_block[:, h * HD : (h + 1) * HD] for h in range(group)], axis=0)
        base = t * (t + 1) // 2

        def scores(j):
            return contract(k[aligned(j * chunk, chunk), :], q_rows, 1, 1)

        def first(j, peak):
            s = scores(j)
            raw[aligned(j * chunk, chunk), :] = s
            return jnp.maximum(peak, fold(s, jnp.max))

        s = scores(t)
        key_at = lax.broadcasted_iota(jnp.int32, (chunk, wide), 0)
        query_at = lax.broadcasted_iota(jnp.int32, (chunk, wide), 1)
        seen = key_at <= (query_at & (TOK - 1)) + y * TOK
        s = jnp.where(seen, s, SMALL)
        raw[aligned(t * chunk, chunk), :] = s
        peak = lax.fori_loop(0, t, first, fold(s, jnp.max))
        peak = jnp.max(peak, axis=0, keepdims=True)
        out[...] = jnp.zeros_like(out)

        def second(j, total):
            e = jnp.exp2((raw[aligned(j * chunk, chunk), :] - peak) * factor)
            rounded = e.astype(BF16)
            kept[base + j] = rounded
            out[...] += jnp.dot(vt[j], rounded, preferred_element_type=F32)
            return total + fold(e, jnp.sum)

        total = lax.fori_loop(0, t + 1, second, jnp.zeros((8, wide), F32))
        scale = 1.0 / jnp.sum(total, axis=0, keepdims=True)
        inverse[t] = jnp.broadcast_to(scale, (8, wide))
        mixed = (out[...] * scale).astype(BF16)
        share = jnp.zeros((TOK, readout.shape[1]), F32)
        for h in range(group):
            at = slice(h * HD, (h + 1) * HD)
            share = share + contract(mixed[:, at], readout[at, :], 0, 0)
        logits[t] = share.astype(BF16)

    loop(0, n.Z, block)


def attend(n, qz, k, v, readout):
    group = qz.shape[2] // HD
    chunk = n.Y * TOK
    wide = group * TOK
    shape = jax.ShapeDtypeStruct
    return pl.pallas_call(
        functools.partial(attend_kernel, n, group),
        out_shape=(
            shape((n.Z, TOK, readout.shape[1]), BF16),
            shape((n.Z * (n.Z + 1) // 2, chunk, wide), BF16),
            shape((n.Z, 8, wide), F32),
        ),
        in_specs=[VMEM] * 4,
        out_specs=(VMEM, VMEM, VMEM),
        scratch_shapes=[
            pltpu.VMEM((n.Z * chunk, wide), F32),
            pltpu.VMEM((n.Z, HD, chunk), BF16),
            pltpu.VMEM((HD, wide), F32),
        ],
        name="attend",
    )(qz, k, v, readout)


def logit_kernel(n, share, base, labels, slopes, arrived, ss, sr, ds, dr):
    seq, dp = place()
    Z, Y = n.Z, n.Y
    z, y = seq // Y, rem(seq, Y)

    def zpeer(d):
        return rem(z + d, Z) * Y + y, dp

    greet(((1, Z, zpeer),))

    def l_send(d):
        to = rem(z + d, Z)
        return send(share.at[to], arrived.at[d], ss.at[d], sr.at[d], to * Y + y, dp)

    loop(1, Z, lambda d: l_send(d).start())
    total = base[...] + share[z].astype(F32)
    for d in range(1, Z):
        l_send(d).wait_recv()
        total = total + arrived[d].astype(F32)
    peak = jnp.max(total, axis=1, keepdims=True)
    e = jnp.exp(total - peak)
    soft = e / jnp.sum(e, axis=1, keepdims=True)
    chosen = labels[...] == lax.broadcasted_iota(jnp.int32, total.shape, 1)
    slopes[z] = (soft - jnp.where(chosen, 1.0, 0.0)).astype(BF16)

    def d_send(d):
        return send(slopes.at[z], slopes.at[z], ds.at[d], dr.at[d], *zpeer(d))

    loop(1, Z, lambda d: d_send(d).start())
    loop(1, Z, lambda d: l_send(d).wait_send())
    loop(1, Z, lambda d: d_send(d).wait())


def logit_slopes(n, share, base, labels):
    dma = pltpu.SemaphoreType.DMA
    return pl.pallas_call(
        functools.partial(logit_kernel, n),
        out_shape=jax.ShapeDtypeStruct(share.shape, BF16),
        in_specs=[VMEM] * 3,
        out_specs=VMEM,
        scratch_shapes=[pltpu.VMEM(share.shape, BF16)] + [dma((n.Z,))] * 4,
        compiler_params=pltpu.CompilerParams(collective_id=1, has_side_effects=True),
        name="logits",
    )(share, base, labels)


def grads_kernel(n, group, slopes, readout, kept, inverse, grads, total):
    chunk = n.Y * TOK
    total[...] = jnp.zeros_like(total)

    def block(t):
        base = t * (t + 1) // 2
        slope = slopes[t]
        parts = []
        for h in range(group):
            at = slice(h * HD, (h + 1) * HD)
            d = contract(slope, readout[at, :], 1, 1)
            column = inverse[t][:, at].T[:, :1]
            parts.append((d * column).astype(BF16))
        d_rows = jnp.concatenate(parts, axis=0)

        def inner(j):
            total[aligned(j * chunk, chunk), :] += jnp.dot(
                kept[base + j], d_rows, preferred_element_type=F32
            )

        loop(0, t + 1, inner)

    loop(0, n.Z, block)

    def put(j):
        for i in range(n.Y):
            grads[i, j] = total[aligned(j * chunk + i * TOK, TOK), :].astype(BF16)

    loop(0, n.Z, put)


def value_grads(n, slopes, readout, kept, inverse):
    group = readout.shape[0] // HD
    return pl.pallas_call(
        functools.partial(grads_kernel, n, group),
        out_shape=jax.ShapeDtypeStruct((n.Y, n.Z, TOK, HD), BF16),
        in_specs=[VMEM] * 4,
        out_specs=VMEM,
        scratch_shapes=[pltpu.VMEM((n.S * TOK, HD), F32)],
        name="value_grads",
    )(slopes, readout, kept, inverse)


def last_kernel(
    n,
    grads,
    cols,
    hessian,
    estimate,
    updated,
    ya,
    dz,
    dv,
    gp,
    gy,
    gz,
    gr,
    y1s,
    y1r,
    z1s,
    z1r,
    xs,
    xr,
    cs,
    cr,
    y2s,
    y2r,
    z2s,
    z2r,
    loc,
):
    seq, dp = place()
    Z, Y, X, C, PP = n.Z, n.Y, n.X, n.C, n.P
    z, y = seq // Y, rem(seq, Y)
    x, c = dp // C, rem(dp, C)
    slot = c * X + x
    rows, feat = hessian.shape

    def zpeer(d):
        return rem(z + d, Z) * Y + y, dp

    def ypeer(e):
        return z * Y + rem(y + e, Y), dp

    def xpeer(d):
        return seq, rem(x + d, X) * C + c

    sibling = x * C + 1 - c
    greet(((1, Z, zpeer), (1, Y, ypeer), (1, X, xpeer), (0, 1, lambda d: (seq, sibling))))

    def y1(e):
        return send(grads.at[rem(y + e, Y)], ya.at[e], y1s.at[e], y1r.at[e], *ypeer(e))

    loop(1, Y, lambda e: y1(e).start())
    loop(1, Y, lambda e: y1(e).wait_recv())

    def z1(d):
        to = rem(z + d, Z)
        dst = dv.at[slot, :, aligned(z * HD, HD)]
        return send(dz.at[to], dst, z1s.at[d], z1r.at[d], to * Y + y, dp)

    def add(to):
        block = grads[y, to].astype(F32)
        for e in range(1, Y):
            block = block + ya[e, to].astype(F32)
        dz[to] = block.astype(BF16)

    def add_send(d):
        add(rem(z + d, Z))
        z1(d).start()

    loop(1, Z, add_send)
    add(z)
    own = pltpu.make_async_copy(dz.at[z], dv.at[slot, :, aligned(z * HD, HD)], loc.at[0])
    own.start()
    own.wait()
    loop(1, Z, lambda d: z1(d).wait_recv())

    def xx(d):
        return send(dv.at[slot], dv.at[slot], xs.at[d], xr.at[d], *xpeer(d))

    def cc(d):
        at = c * X + rem(x - d + X, X)
        return send(dv.at[at], dv.at[at], cs.at[d], cr.at[d], seq, sibling)

    loop(1, X, lambda d: xx(d).start())
    cc(0).start()

    def on(d):
        xx(d).wait_recv()
        cc(d).start()

    loop(1, X, on)
    loop(0, X, lambda d: cc(d).wait_recv())

    tokens = PP * TOK
    right = cols[...].reshape(tokens, feat)
    wide = min(512, dv.shape[2])
    heads = wide // HD

    def product(i):
        left = dv[:, :, aligned(i * wide, wide)].reshape(tokens, wide)
        g = contract(left, right, 0, 0).astype(BF16).reshape(heads, Y, rows, feat)
        for a in range(heads):
            for b in range(Y):
                gp[b, i * heads + a] = g[a, b]

    loop(0, dv.shape[2] // wide, product)

    def y2(e):
        return send(gp.at[rem(y + e, Y)], gy.at[e], y2s.at[e], y2r.at[e], *ypeer(e))

    loop(1, Y, lambda e: y2(e).start())
    loop(1, Y, lambda e: y2(e).wait_recv())

    def z2(d):
        to = rem(z + d, Z)
        return send(gz.at[to], gr.at[d], z2s.at[d], z2r.at[d], to * Y + y, dp)

    def sum_at(to):
        block = gp[y, to].astype(F32)
        for e in range(1, Y):
            block = block + gy[e, to].astype(F32)
        return block

    def sum_send(d):
        to = rem(z + d, Z)
        gz[to] = sum_at(to).astype(BF16)
        z2(d).start()

    loop(1, Z, sum_send)
    total = sum_at(z)
    for d in range(1, Z):
        z2(d).wait_recv()
        total = total + gr[d].astype(F32)
    fresh = total * total / (n.S * TOK * PP)
    estimate[...] = fresh
    updated[...] = beta_two * hessian[...] + (1.0 - beta_two) * fresh

    loop(1, Y, lambda e: y1(e).wait_send())
    loop(1, Z, lambda d: z1(d).wait_send())
    loop(1, X, lambda d: xx(d).wait_send())
    loop(0, X, lambda d: cc(d).wait_send())
    loop(1, Y, lambda e: y2(e).wait_send())
    loop(1, Z, lambda d: z2(d).wait_send())


def last(n, grads, cols, hessian):
    dma = pltpu.SemaphoreType.DMA
    rows, feat = hessian.shape
    kv = n.Z * HD
    out = jax.ShapeDtypeStruct(hessian.shape, F32)
    return pl.pallas_call(
        functools.partial(last_kernel, n),
        out_shape=(out, out),
        in_specs=[VMEM] * 3,
        out_specs=(VMEM, VMEM),
        scratch_shapes=[
            pltpu.VMEM((n.Y, n.Z, TOK, HD), BF16),
            pltpu.VMEM((n.Z, TOK, HD), BF16),
            pltpu.VMEM((n.P, TOK, kv), BF16),
            pltpu.VMEM((n.Y, n.Z, rows, feat), BF16),
            pltpu.VMEM((n.Y, n.Z, rows, feat), BF16),
            pltpu.VMEM((n.Z, rows, feat), BF16),
            pltpu.VMEM((n.Z, rows, feat), BF16),
            dma((n.Y,)),
            dma((n.Y,)),
            dma((n.Z,)),
            dma((n.Z,)),
            dma((n.X,)),
            dma((n.X,)),
            dma((n.X,)),
            dma((n.X,)),
            dma((n.Y,)),
            dma((n.Y,)),
            dma((n.Z,)),
            dma((n.Z,)),
            dma((1,)),
        ],
        compiler_params=pltpu.CompilerParams(collective_id=2, has_side_effects=True),
        name="last",
    )(grads, cols, hessian)


def local(queries, keys, hidden, value_weight, readout, base_logits, labels, hessian):
    n = sizes_of(lax.axis_size("seq"), lax.axis_size("dp"))
    cols, qz, kz, vz = front(n, hidden[0], queries[0], keys[0], value_weight)
    z = lax.axis_index("seq") // n.Y
    mine = lax.dynamic_slice_in_dim(readout, z * qz.shape[2], qz.shape[2], 0)
    share, kept, inverse = attend(n, qz, kz.reshape(-1, HD), vz.reshape(-1, HD), mine)
    slopes = logit_slopes(n, share, base_logits[0], labels.reshape(TOK, 1))
    grads = value_grads(n, slopes, mine, kept, inverse)
    return last(n, grads, cols, hessian)


def solution(mesh):
    placed = (
        P("dp", "seq", None),
        P("dp", "seq", None),
        P("dp", "seq", None),
        P("dp", None),
        P(),
        P("dp", "seq", None),
        P("dp", "seq"),
        P("seq", "dp"),
    )
    return jax.shard_map(
        local,
        mesh=mesh,
        in_specs=placed,
        out_specs=(P("seq", "dp"), P("seq", "dp")),
        check_vma=False,
    )
```

time: 697 us -> 225 us (0.32); the launches traced: 689 us -> 225 us
  Pallas kernels: 0 us -> 218 us
  matrix products: 172 us -> 0 us
  blocking collectives: 170 us -> 0 us
  local copies, waits for them, and re-layouts: 118 us -> 5.98 us
  waiting for transfers between devices: 96.7 us -> 0 us
  other arithmetic: 78 us -> 0 us
  starting transfers between devices: 49.3 us -> 0 us
    pallas_call x0 -> x5, Pallas kernels: none -> 218 us  [the longest x1 70.6 us: last(): pl.pallas_call(functools.partial(last_kernel, n), out_shape=(out, out), i...]
    dot_general x112 -> x0, matrix products: 172 us -> none  [the longest x36 61.3 us: attend_inner(): jnp.einsum('hqk,hkd->hqd', weights, v_block, preferred_element_type=jnp.f...]
    all_to_all x6 -> x0, blocking collectives: 170 us -> none  [the longest x3 72.8 us: several_exchanges(): lax.all_to_all(share, axis, split_axis=0, concat_axis=0, tiled=True)]
    all_to_all x7 -> x0, waiting for transfers between devices: 96.7 us -> none  [the longest x5 62.1 us: several_exchanges(): lax.all_to_all(share, axis, split_axis=0, concat_axis=0, tiled=True)]
    all_to_all x7 -> x0, starting transfers between devices: 49.3 us -> none  [the longest x5 34.4 us: several_exchanges(): lax.all_to_all(share, axis, split_axis=0, concat_axis=0, tiled=True)]
    unnamed x2 -> x0, other arithmetic: 46.7 us -> none
    dynamic_slice x68 -> x1, local copies, waits for them, and re-layouts: 38.4 us -> 0.72 us  [local(): mine = lax.dynamic_slice_in_dim(readout, z * qz.shape[2], qz.shape[2], 0)]
    unnamed x27 -> x6, local copies, waits for them, and re-layouts: 33.9 us -> 4.52 us
  transfers between devices with their start and end apart: 7 -> 0, of which waited for: 7 -> 0; matrix products, arithmetic and copies ran while one was open for 4% -> 0% of each run, Pallas kernels for 0% -> 0%
where the time goes in v1:
time: 225 us
  Pallas kernels  218 us (97%)
  local copies, waits for them, and re-layouts  5.98 us (3%)
    pallas_call x1, Pallas kernels, last(): pl.pallas_call(functools.partial(last_kernel, n), out_shape=(out, out), i...  70.6 us
    pallas_call x1, Pallas kernels, front(): pl.pallas_call(functools.partial(front_kernel, n), out_shape=(shape((n.P,...  63 us
    pallas_call x1, Pallas kernels, attend(): pl.pallas_call(functools.partial(attend_kernel, n, group), out_shape=(sha...  34.9 us
    pallas_call x1, Pallas kernels, logit_slopes(): pl.pallas_call(functools.partial(logit_kernel, n), out_shape=jax.ShapeDty...  28.9 us
    pallas_call x1, Pallas kernels, value_grads(): pl.pallas_call(functools.partial(grads_kernel, n, group), out_shape=jax.S...  20.7 us
    unnamed x6, local copies, waits for them, and re-layouts  4.52 us

profile of v1, /device:TPU:1, one launch (start us, length us, event | category | flops | bytes accessed | tf_op | source)
XLA Modules:
  0.0 224.8 jit_solution(6368795877897701686)
XLA Ops:
  0.6 0.0 copy-start
  0.7 1.6 copy-done
  2.2 0.7 constant_dynamic-slice_fusion.readout
  2.9 63.0 %front.1 = (bf16[8,128,512]{2,1,0:T(8,128)(2,1)}, bf16[8,128,512]{2,1,0:T(8,128)(2,1)}, bf16[32,128,128]{2,1,0:T(8,128)(2,1)}, bf16[32,128,128]{2,1,0:T(8,128)(2,1)}) custom-call(bf16[128,4096]{1,0:T(8,128)(2,1)} %bitcast.7, bf16[128,4096]{1,0:T(8,128)(2,1)} %bitcast.8, bf16[128,1024]{1,0:T(8,128)(2,1)} %bitcast.11, bf16[512,1024]{1,0:T(8,128)(2,1)} %weight.1), custom_call_target="tpu_custom_call" | custom-call | tf_op jit(solution)/shard_map/front/pallas_call | solution.py:247
  66.0 0.0 copy-start.1
  66.0 34.9 %attend.1 = (bf16[8,128,256]{2,1,0:T(8,128)(2,1)}, bf16[36,512,512]{2,1,0:T(8,128)(2,1)}, f32[8,8,512]{2,1,0:T(8,128)}) custom-call(bf16[8,128,512]{2,1,0:T(8,128)(2,1)} %get-tuple-element.9.qz, bf16[4096,128]{1,0:T(8,128)(2,1)} %bitcast.9, bf16[4096,128]{1,0:T(8,128)(2,1)} %bitcast.10, bf16[512,256]{1,0:T(8,128)(2,1)} %constant_dynamic-slice_fusion.readout), custom_call_target="tpu_custom_call" | custom-call | tf_op jit(solution)/shard_map/attend/pallas_call | solution.py:352
  100.8 0.0 copy-done.1
  100.8 0.7 copy.10.labels
  101.6 28.9 %logits.1.slopes = bf16[8,128,256]{2,1,0:T(8,128)(2,1)} custom-call(bf16[8,128,256]{2,1,0:T(8,128)(2,1)} %get-tuple-element.12.share, f32[128,256]{1,0:T(8,128)} %bitcast.12, s32[128,1]{1,0:T(8,128)} %copy.10.labels), custom_call_target="tpu_custom_call" | custom-call | tf_op jit(solution)/shard_map/logits/pallas_call | solution.py:405
  130.5 20.7 %value_grads.1.grads = bf16[4,8,128,128]{3,2,1,0:T(8,128)(2,1)} custom-call(bf16[8,128,256]{2,1,0:T(8,128)(2,1)} %logits.1.slopes, bf16[512,256]{1,0:T(8,128)(2,1)} %constant_dynamic-slice_fusion.readout, bf16[36,512,512]{2,1,0:T(8,128)(2,1)} %get-tuple-element.13.kept, f32[8,8,512]{2,1,0:T(8,128)} %get-tuple-element.14.inverse), custom_call_target="tpu_custom_call" | custom-call | tf_op jit(solution)/shard_map/value_grads/pallas_call | solution.py:449
  151.3 70.6 %last.1 = (f32[32,512]{1,0:T(8,128)}, f32[32,512]{1,0:T(8,128)}) custom-call(bf16[4,8,128,128]{3,2,1,0:T(8,128)(2,1)} %value_grads.1.grads, bf16[8,128,512]{2,1,0:T(8,128)(2,1)} %get-tuple-element.15.cols, f32[32,512]{1,0:T(8,128)} %hessian.1), custom_call_target="tpu_custom_call" | custom-call | tf_op jit(solution)/shard_map/last/pallas_call | solution.py:608
  221.8 1.5 copy.13
  223.3 1.5 copy.14
Async XLA Ops:
  0.6 1.6 copy-start
  66.0 34.9 %copy-start.1 = (s32[1,128]{1,0:T(1,128)S(1)}, s32[1,128]{1,0:T(1,128)}, u32[]{:S(2)}) copy-start(s32[1,128]{1,0:T(1,128)} %param.14) | copy-start | bytes 1540

commit v2 on v0

v2 whole, which is shorter than its diff:
```python
import functools
import math
import types

import jax
import jax.numpy as jnp
from jax import lax
from jax.experimental import pallas as pl
from jax.experimental.pallas import tpu as pltpu
from jax.sharding import PartitionSpec as P

HD = 128
TOK = 128
SMALL = -1.0e30
beta_two = 0.99
MESH = pl.DeviceIdType.MESH
F32 = jnp.float32
BF16 = jnp.bfloat16
VMEM = pl.BlockSpec(memory_space=pltpu.VMEM)
ANY = pl.BlockSpec(memory_space=pl.ANY)


def sizes_of(seq, dp):
    n = types.SimpleNamespace(S=seq, P=dp, C=2, X=dp // 2)
    n.Y = 4 if seq == 32 else 2
    n.Z = seq // n.Y
    return n


def place():
    return lax.axis_index("seq"), lax.axis_index("dp")


def rem(a, b):
    return lax.rem(a, jnp.int32(b))


def loop(low, high, step):
    def body(i, carry):
        step(i)
        return carry

    lax.fori_loop(low, high, body, 0)


def aligned(start, size):
    return pl.ds(pl.multiple_of(start, size), size)


def send(src, dst, send_sem, recv_sem, seq, dp):
    return pltpu.make_async_remote_copy(
        src_ref=src,
        dst_ref=dst,
        send_sem=send_sem,
        recv_sem=recv_sem,
        device_id=(seq, dp),
        device_id_type=MESH,
    )


def greet(peers):
    barrier = pltpu.get_barrier_semaphore()
    count = 0
    for low, high, where in peers:

        def one(d, where=where):
            seq, dp = where(d)
            pl.semaphore_signal(barrier, inc=1, device_id=(seq, dp), device_id_type=MESH)

        loop(low, high, one)
        count += high - low
    pl.semaphore_wait(barrier, count)


def contract(a, b, da, db):
    return lax.dot_general(a, b, (((da,), (db,)), ((), ())), preferred_element_type=F32)


def whole_kernel(n, names, hidden, queries, keys, weight_in, readout_in, base, labels, result, *scratch):
    r = types.SimpleNamespace(**dict(zip(names, scratch, strict=True)))
    seq, dp = place()
    Z, Y, X, C, PP = n.Z, n.Y, n.X, n.C, n.P
    z, y = seq // Y, rem(seq, Y)
    x, c = dp // C, rem(dp, C)
    feat = hidden.shape[1] // PP
    qw = queries.shape[1] // Z
    kv = keys.shape[1]
    group = qw // HD
    chunk = Y * TOK
    wide = group * TOK
    sibling = x * C + 1 - c
    slot = c * X + x

    def zpeer(d):
        return rem(z + d, Z) * Y + y, dp

    def ypeer(e):
        return z * Y + rem(y + e, Y), dp

    def ppeer(d):
        return seq, rem(dp + d, PP)

    def xpeer(d):
        return seq, rem(x + d, X) * C + c

    def lanes(ref, i, width):
        return ref.at[:, aligned(i * width, width)]

    get_weight = pltpu.make_async_copy(weight_in, r.weight, r.loc.at[4])
    get_readout = pltpu.make_async_copy(readout_in.at[aligned(z * qw, qw)], r.readout, r.loc.at[5])
    own_k = pltpu.make_async_copy(lanes(keys, z, HD), r.kz.at[seq], r.loc.at[0])
    own_h = pltpu.make_async_copy(lanes(hidden, dp, feat), r.cols.at[slot], r.loc.at[1])
    own_q = pltpu.make_async_copy(lanes(queries, z, qw), r.qz.at[z], r.loc.at[2])
    for own in (own_k, own_h, own_q, get_weight, get_readout):
        own.start()

    greet(((1, Z, zpeer), (1, Y, ypeer), (1, PP, ppeer)))


    def k_send(d):
        to = rem(z + d, Z)
        return send(lanes(keys, to, HD), r.kz.at[seq], r.ks.at[d], r.kr.at[d], to * Y + y, dp)

    def h_send(d):
        to = rem(dp + d, PP)
        return send(lanes(hidden, to, feat), r.cols.at[slot], r.hs.at[d], r.hr.at[d], seq, to)

    def q_send(d):
        to = rem(z + d, Z)
        return send(lanes(queries, to, qw), r.qz.at[z], r.qs.at[d], r.qr.at[d], to * Y + y, dp)

    loop(1, Z, lambda d: k_send(d).start())
    loop(1, PP, lambda d: h_send(d).start())
    loop(1, Z, lambda d: q_send(d).start())

    def forward(ref, first, d, e, ssem, rsem):
        at = rem(z - d + Z, Z) * Y + y
        src = first if first is not None else ref.at[at]
        return send(src, ref.at[at], ssem.at[d, e], rsem.at[d, e], *ypeer(e))

    def k_forward(first, d, e):
        return forward(r.kz, first, d, e, r.kys, r.kyr)

    def v_forward(first, d, e):
        return forward(r.vz, first, d, e, r.vys, r.vyr)

    def v_send(d):
        to = rem(z + d, Z)
        return send(lanes(r.val, to, HD), r.vz.at[seq], r.vs.at[d], r.vr.at[d], to * Y + y, dp)

    def pass_on(sent, via, d):
        sent(d).wait_recv()
        loop(1, Y, lambda e: via(None, d, e).start())

    k_mine = lanes(keys, z, HD)
    v_mine = lanes(r.val, z, HD)
    loop(1, Y, lambda e: k_forward(k_mine, 0, e).start())
    loop(1, Z, lambda d: pass_on(k_send, k_forward, d))


    get_weight.wait()
    own_h.wait()
    loop(1, PP, lambda d: h_send(d).wait_recv())
    rows = X * TOK
    width = min(512, kv)

    def product(half):
        block = r.cols[pl.ds(half * X, X)].reshape(rows, feat)

        def piece(w):
            r.part[aligned(half * rows, rows), aligned(w * width, width)] = jnp.dot(
                block, r.weight[:, aligned(w * width, width)], preferred_element_type=F32
            ).astype(BF16)

        loop(0, kv // width, piece)

    other = 1 - c

    def c_send(i):
        row = aligned((other * X + i) * TOK, TOK)
        return send(r.part.at[row], r.pair.at[i], r.cs.at[i], r.cr.at[i], seq, sibling)

    product(other)
    loop(0, X, lambda i: c_send(i).start())
    product(c)

    def x_send(d):
        to = rem(x + d, X)
        return send(r.both.at[to], r.xin.at[d], r.xs.at[d], r.xr.at[d], seq, to * C + c)

    def join(d):
        to = rem(x + d, X)
        c_send(to).wait_recv()
        mine = r.part[aligned((c * X + to) * TOK, TOK)].astype(F32)
        r.both[to] = (mine + r.pair[to].astype(F32)).astype(BF16)

    def join_send(d):
        join(d)
        x_send(d).start()

    def join_all():
        loop(1, X, join_send)
        join(jnp.int32(X))

    own_v = pltpu.make_async_copy(v_mine, r.vz.at[seq], r.loc.at[3])

    def values_out():
        total = r.both[x].astype(F32)
        for d in range(1, X):
            x_send(d).wait_recv()
            total = total + r.xin[d].astype(F32)
        r.val[...] = total.astype(BF16)
        loop(1, Z, lambda d: v_send(d).start())
        own_v.start()
        loop(1, Y, lambda e: v_forward(v_mine, 0, e).start())


    own_k.wait()
    own_q.wait()
    loop(1, Y, lambda e: k_forward(k_mine, 0, e).wait_recv())
    loop(1, Z, lambda d: loop(1, Y, lambda e: k_forward(None, d, e).wait_recv()))
    factor = math.log2(math.e) / math.sqrt(HD)

    def fold(a, op):
        return op(a.reshape(chunk // 8, 8, wide), axis=0)

    def keys_of(j):
        return r.kz[pl.ds(j * Y, Y)].reshape(chunk, HD)

    def weights_of(t):
        q_block = r.qz[t]
        q_rows = jnp.concatenate([q_block[:, h * HD : (h + 1) * HD] for h in range(group)], axis=0)
        at = t * (t + 1) // 2

        def first(j, peak):
            s = contract(keys_of(j), q_rows, 1, 1)
            r.raw[aligned(j * chunk, chunk), :] = s
            return jnp.maximum(peak, fold(s, jnp.max))

        s = contract(keys_of(t), q_rows, 1, 1)
        key_at = lax.broadcasted_iota(jnp.int32, (chunk, wide), 0)
        query_at = lax.broadcasted_iota(jnp.int32, (chunk, wide), 1)
        s = jnp.where(key_at <= (query_at & (TOK - 1)) + y * TOK, s, SMALL)
        r.raw[aligned(t * chunk, chunk), :] = s
        peak = lax.fori_loop(0, t, first, fold(s, jnp.max))
        peak = jnp.max(peak, axis=0, keepdims=True)

        def second(j, total):
            e = jnp.exp2((r.raw[aligned(j * chunk, chunk), :] - peak) * factor)
            r.kept[at + j] = e.astype(BF16)
            return total + fold(e, jnp.sum)

        total = lax.fori_loop(0, t + 1, second, jnp.zeros((8, wide), F32))
        scale = 1.0 / jnp.sum(total, axis=0, keepdims=True)
        r.inverse[t] = jnp.broadcast_to(scale, (8, wide))

    steps = {}
    steps.setdefault(min(1, Z - 1), []).append(join_all)
    steps.setdefault(min(3, Z - 1), []).append(values_out)

    def score_step(d):
        @pl.when(d > 0)
        def _():
            q_send(d).wait_recv()

        weights_of(rem(z - d + Z, Z))
        for at, calls in steps.items():

            @pl.when(d == at)
            def _(calls=calls):
                for call in calls:
                    call()

    early = max(1, Z - 2)
    loop(0, early, score_step)
    if early <= 3 and Z - 1 >= early:
        loop(early, Z, score_step)
        loop(1, Z, lambda d: pass_on(v_send, v_forward, d))
    else:
        loop(1, Z, lambda d: pass_on(v_send, v_forward, d))
        loop(early, Z, score_step)


    get_readout.wait()
    own_v.wait()
    loop(1, Y, lambda e: v_forward(v_mine, 0, e).wait_recv())
    loop(1, Z, lambda d: loop(1, Y, lambda e: v_forward(None, d, e).wait_recv()))

    def turn(j):
        r.vt[j] = r.vz[pl.ds(j * Y, Y)].reshape(chunk, HD).astype(F32).T.astype(BF16)

    loop(0, Z, turn)

    def l_send(d):
        to = rem(z + d, Z)
        return send(r.share.at[to], r.arrived.at[d], r.ls.at[d], r.lr.at[d], to * Y + y, dp)

    def share_step(i):
        t = rem(z + i, Z)
        at = t * (t + 1) // 2
        r.out[...] = jnp.zeros_like(r.out)

        def add(j):
            r.out[...] += jnp.dot(r.vt[j], r.kept[at + j], preferred_element_type=F32)

        loop(0, t + 1, add)
        mixed = (r.out[...] * r.inverse[t][:1]).astype(BF16)
        part = jnp.zeros((TOK, r.readout.shape[1]), F32)
        for h in range(group):
            at = slice(h * HD, (h + 1) * HD)
            part = part + contract(mixed[:, at], r.readout[at, :], 0, 0)
        r.share[t] = part.astype(BF16)

        @pl.when(i < Z)
        def _():
            l_send(i).start()

    loop(1, Z + 1, share_step)

    total = base[...] + r.share[z].astype(F32)
    for d in range(1, Z):
        l_send(d).wait_recv()
        total = total + r.arrived[d].astype(F32)
    peak = jnp.max(total, axis=1, keepdims=True)
    e = jnp.exp(total - peak)
    soft = e / jnp.sum(e, axis=1, keepdims=True)
    label = jnp.broadcast_to(labels[...].astype(F32), (8, TOK)).T[:, :1]
    column = lax.broadcasted_iota(jnp.int32, total.shape, 1).astype(F32)
    r.slopes[z] = (soft - jnp.where(label == column, 1.0, 0.0)).astype(BF16)

    def s_send(d):
        return send(r.slopes.at[z], r.slopes.at[z], r.ss.at[d], r.sr.at[d], *zpeer(d))

    loop(1, Z, lambda d: s_send(d).start())

    def slope_step(d):
        @pl.when(d > 0)
        def _():
            s_send(d).wait_recv()

        t = rem(z - d + Z, Z)
        slope = r.slopes[t]
        for h in range(group):
            at = slice(h * HD, (h + 1) * HD)
            column = r.inverse[t][:, at].T[:, :1]
            r.d_rows[t, at, :] = (contract(slope, r.readout[at, :], 1, 1) * column).astype(BF16)

    loop(0, Z, slope_step)


    tokens = PP * TOK
    quarter = HD // Y

    def head_lanes(ref, h):
        return ref.at[:, aligned(h * HD, HD)]

    def y1(i, e):
        to = rem(y + e, Y)
        return send(r.grads.at[i, to], r.ya.at[i, e], r.y1s.at[i, e], r.y1r.at[i, e], *ypeer(e))

    def stage0(i):
        j = rem(z + i, Z)
        r.acc[...] = jnp.zeros_like(r.acc)

        def add(t):
            r.acc[...] += jnp.dot(
                r.kept[t * (t + 1) // 2 + j], r.d_rows[t], preferred_element_type=F32
            )

        loop(j, Z, add)
        for b in range(Y):
            r.grads[i, b] = r.acc[b * TOK : (b + 1) * TOK, :].astype(BF16)
        loop(1, Y, lambda e: y1(i, e).start())

    def z1(i):
        to = rem(z + i, Z)
        dst = head_lanes(r.dv.at[slot], z)
        return send(r.dz.at[i], dst, r.z1s.at[i], r.z1r.at[i], to * Y + y, dp)

    own_dv = pltpu.make_async_copy(r.dz.at[Z], head_lanes(r.dv.at[slot], z), r.loc.at[6])

    def stage1(i):
        loop(1, Y, lambda e: y1(i, e).wait_recv())
        block = r.grads[i, y].astype(F32)
        for e in range(1, Y):
            block = block + r.ya[i, e].astype(F32)
        r.dz[i] = block.astype(BF16)

        @pl.when(i < Z)
        def _():
            z1(i).start()

        @pl.when(i == Z)
        def _():
            own_dv.start()

    def head_at(i):
        return rem(z - i + Z, Z)

    def xx(i, d):
        ref = head_lanes(r.dv.at[slot], head_at(i))
        return send(ref, ref, r.x2s.at[i, d], r.x2r.at[i, d], *xpeer(d))

    def cc(i, d):
        at = c * X + rem(x - d + X, X)
        ref = head_lanes(r.dv.at[at], head_at(i))
        return send(ref, ref, r.c2s.at[i, d], r.c2r.at[i, d], seq, sibling)

    def stage2(i):
        @pl.when(i < Z)
        def _():
            z1(i).wait_recv()

        @pl.when(i == Z)
        def _():
            own_dv.wait()

        loop(1, X, lambda d: xx(i, d).start())
        cc(i, 0).start()

    def stage3(i):
        def on(d):
            xx(i, d).wait_recv()
            cc(i, d).start()

        loop(1, X, on)

    def y2(i, e):
        to = rem(y + e, Y)
        return send(r.gp.at[i, to], r.gy.at[i, e], r.y2s.at[i, e], r.y2r.at[i, e], *ypeer(e))

    def stage4(i):
        loop(0, X, lambda d: cc(i, d).wait_recv())
        left = r.dv[:, :, aligned(head_at(i) * HD, HD)].reshape(tokens, HD)
        right = r.cols[...].reshape(tokens, feat)
        r.gp[i] = contract(left, right, 0, 0).astype(BF16).reshape(Y, quarter, feat)
        loop(1, Y, lambda e: y2(i, e).start())

    def z2(i):
        return send(r.gz.at[i], r.gr.at[i], r.z2s.at[i], r.z2r.at[i], head_at(i) * Y + y, dp)

    def stage5(i):
        loop(1, Y, lambda e: y2(i, e).wait_recv())
        block = r.gp[i, y].astype(F32)
        for e in range(1, Y):
            block = block + r.gy[i, e].astype(F32)

        @pl.when(i < Z)
        def _():
            r.gz[i] = block.astype(BF16)
            z2(i).start()

        @pl.when(i == Z)
        def _():
            r.own[...] = block

    r.sum[...] = jnp.zeros_like(r.sum)

    def stage6(i):
        @pl.when(i < Z)
        def _():
            z2(i).wait_recv()
            r.sum[...] += r.gr[i].astype(F32)

    stages = (stage0, stage1, stage2, stage3, stage4, stage5, stage6)

    def tick(k):
        for s, stage in enumerate(stages):

            @pl.when((k - s >= 1) & (k - s <= Z))
            def _(s=s, stage=stage):
                stage(k - s)

    loop(1, Z + len(stages), tick)
    result[...] = r.sum[...] + r.own[...]


    def drain(i):
        loop(1, Y, lambda e: k_forward(None, i, e).wait_send())
        loop(1, Y, lambda e: v_forward(None, i, e).wait_send())
        for sent in (k_send, q_send, v_send, l_send, s_send, z1, z2):
            sent(i).wait_send()

    loop(1, Z, drain)
    loop(1, Y, lambda e: k_forward(k_mine, 0, e).wait_send())
    loop(1, Y, lambda e: v_forward(v_mine, 0, e).wait_send())
    loop(1, PP, lambda d: h_send(d).wait_send())
    loop(0, X, lambda i: c_send(i).wait_send())
    loop(1, X, lambda d: x_send(d).wait_send())

    def drain_late(i):
        loop(1, Y, lambda e: y1(i, e).wait_send())
        loop(1, Y, lambda e: y2(i, e).wait_send())
        loop(1, X, lambda d: xx(i, d).wait_send())
        loop(0, X, lambda d: cc(i, d).wait_send())

    loop(1, Z + 1, drain_late)


def whole(n, hidden, queries, keys, weight, readout, base, labels, rows):
    Z, Y, X, PP = n.Z, n.Y, n.X, n.P
    feat = hidden.shape[1] // PP
    qw = queries.shape[1] // Z
    kv = keys.shape[1]
    cand = readout.shape[1]
    chunk = Y * TOK
    dma = pltpu.SemaphoreType.DMA
    vmem = pltpu.VMEM
    scratch = dict(
        weight=vmem((feat, kv), BF16),
        readout=vmem((qw, cand), BF16),
        cols=vmem((PP, TOK, feat), BF16),
        qz=vmem((Z, TOK, qw), BF16),
        kz=vmem((n.S, TOK, HD), BF16),
        vz=vmem((n.S, TOK, HD), BF16),
        part=vmem((PP * TOK, kv), BF16),
        pair=vmem((X, TOK, kv), BF16),
        both=vmem((X, TOK, kv), BF16),
        xin=vmem((X, TOK, kv), BF16),
        val=vmem((TOK, kv), BF16),
        raw=vmem((Z * chunk, qw), F32),
        vt=vmem((Z, HD, chunk), BF16),
        out=vmem((HD, qw), F32),
        kept=vmem((Z * (Z + 1) // 2, chunk, qw), BF16),
        inverse=vmem((Z, 8, qw), F32),
        share=vmem((Z, TOK, cand), BF16),
        arrived=vmem((Z, TOK, cand), BF16),
        slopes=vmem((Z, TOK, cand), BF16),
        d_rows=vmem((Z, qw, HD), BF16),
        acc=vmem((chunk, HD), F32),
        grads=vmem((Z + 1, Y, TOK, HD), BF16),
        ya=vmem((Z + 1, Y, TOK, HD), BF16),
        dz=vmem((Z + 1, TOK, HD), BF16),
        dv=vmem((PP, TOK, kv), BF16),
        gp=vmem((Z + 1, Y, rows, feat), BF16),
        gy=vmem((Z + 1, Y, rows, feat), BF16),
        gz=vmem((Z, rows, feat), BF16),
        gr=vmem((Z, rows, feat), BF16),
        sum=vmem((rows, feat), F32),
        own=vmem((rows, feat), F32),
        loc=dma((7,)),
    )
    for name in ("h",):
        scratch |= {name + "s": dma((PP,)), name + "r": dma((PP,))}
    for name in ("k", "q", "v", "l", "s", "z1", "z2"):
        scratch |= {name + "s": dma((Z,)), name + "r": dma((Z,))}
    for name in ("c", "x"):
        scratch |= {name + "s": dma((X,)), name + "r": dma((X,))}
    for name in ("ky", "vy"):
        scratch |= {name + "s": dma((Z, Y)), name + "r": dma((Z, Y))}
    for name in ("y1", "y2"):
        scratch |= {name + "s": dma((Z + 1, Y)), name + "r": dma((Z + 1, Y))}
    for name in ("x2", "c2"):
        scratch |= {name + "s": dma((Z + 1, X)), name + "r": dma((Z + 1, X))}
    return pl.pallas_call(
        functools.partial(whole_kernel, n, tuple(scratch)),
        out_shape=jax.ShapeDtypeStruct((rows, feat), F32),
        in_specs=[ANY, ANY, ANY, ANY, ANY, VMEM, VMEM],
        out_specs=VMEM,
        scratch_shapes=list(scratch.values()),
        compiler_params=pltpu.CompilerParams(
            collective_id=0, has_side_effects=True, vmem_limit_bytes=64 * 1024 * 1000
        ),
        name="whole",
    )(hidden, queries, keys, weight, readout, base, labels)


def local(queries, keys, hidden, value_weight, readout, base_logits, labels, hessian):
    n = sizes_of(lax.axis_size("seq"), lax.axis_size("dp"))
    total = whole(
        n,
        hidden[0],
        queries[0],
        keys[0],
        value_weight,
        readout,
        base_logits[0],
        labels,
        hessian.shape[0],
    )
    estimate = total * total / (n.S * TOK * n.P)
    return estimate, beta_two * hessian + (1.0 - beta_two) * estimate


def solution(mesh):
    placed = (
        P("dp", "seq", None),
        P("dp", "seq", None),
        P("dp", "seq", None),
        P("dp", None),
        P(),
        P("dp", "seq", None),
        P("dp", "seq"),
        P("seq", "dp"),
    )
    return jax.shard_map(
        local,
        mesh=mesh,
        in_specs=placed,
        out_specs=(P("seq", "dp"), P("seq", "dp")),
        check_vma=False,
    )
```

time: 697 us -> 155 us (0.22); the launches traced: 689 us -> 155 us
  matrix products: 172 us -> 0 us
  blocking collectives: 170 us -> 0 us
  Pallas kernels: 0 us -> 153 us
  local copies, waits for them, and re-layouts: 118 us -> 0.01 us
  waiting for transfers between devices: 96.7 us -> 0 us
  other arithmetic: 78 us -> 1.51 us
  starting transfers between devices: 49.3 us -> 0 us
    dot_general x112 -> x0, matrix products: 172 us -> none  [the longest x36 61.3 us: attend_inner(): jnp.einsum('hqk,hkd->hqd', weights, v_block, preferred_element_type=jnp.f...]
    all_to_all x6 -> x0, blocking collectives: 170 us -> none  [the longest x3 72.8 us: several_exchanges(): lax.all_to_all(share, axis, split_axis=0, concat_axis=0, tiled=True)]
    pallas_call x0 -> x1, Pallas kernels: none -> 153 us  [whole(): pl.pallas_call(functools.partial(whole_kernel, n, tuple(scratch)), out_sh...]
    all_to_all x7 -> x0, waiting for transfers between devices: 96.7 us -> none  [the longest x5 62.1 us: several_exchanges(): lax.all_to_all(share, axis, split_axis=0, concat_axis=0, tiled=True)]
    all_to_all x7 -> x0, starting transfers between devices: 49.3 us -> none  [the longest x5 34.4 us: several_exchanges(): lax.all_to_all(share, axis, split_axis=0, concat_axis=0, tiled=True)]
    unnamed x2 -> x0, other arithmetic: 46.7 us -> none
    dynamic_slice x68 -> x0, local copies, waits for them, and re-layouts: 38.4 us -> none  [the longest x36 25.4 us: value_inner(): total_block = lax.dynamic_slice_in_dim(total, i * width, width, 1)]
    unnamed x27 -> x2, local copies, waits for them, and re-layouts: 33.9 us -> 0.01 us
  transfers between devices with their start and end apart: 7 -> 0, of which waited for: 7 -> 0; matrix products, arithmetic and copies ran while one was open for 4% -> 0% of each run, Pallas kernels for 0% -> 0%
where the time goes in v2:
time: 155 us
  Pallas kernels  153 us (99%)
    pallas_call x1, Pallas kernels, whole(): pl.pallas_call(functools.partial(whole_kernel, n, tuple(scratch)), out_sh...  153 us

profile of v2, /device:TPU:1, one launch (start us, length us, event | category | flops | bytes accessed | tf_op | source)
XLA Modules:
  0.0 154.8 jit_solution(8624894676407611506)
XLA Ops:
  0.6 0.0 copy-start
  0.6 152.6 %whole.1 = f32[32,512]{1,0:T(8,128)} custom-call(bf16[128,4096]{1,0:T(8,128)(2,1)} %bitcast.4, bf16[128,4096]{1,0:T(8,128)(2,1)} %bitcast.5, bf16[128,1024]{1,0:T(8,128)(2,1)} %bitcast.6, bf16[512,1024]{1,0:T(8,128)(2,1)} %weight_in.1, bf16[4096,256]{1,0:T(8,128)(2,1)} %readout_in.1, f32[128,256]{1,0:T(8,128)} %bitcast.7, s32[1,128]{1,0:T(1,128)} %labels.1), custom_call_target="tpu_custom_call" | custom-call | tf_op jit(solution)/shard_map/whole/pallas_call | solution.py:555
  153.3 0.0 copy-done
  153.3 1.5 multiply_add_fusion
Async XLA Ops:
  0.6 152.6 %copy-start = (f32[32,512]{1,0:T(8,128)S(1)}, f32[32,512]{1,0:T(8,128)}, u32[]{:S(2)}) copy-start(f32[32,512]{1,0:T(8,128)} %param.15) | copy-start | bytes 196612

commit v3 on v2

--- a/solution.py
+++ b/solution.py
@@ -145,15 +145,14 @@
         return forward(r.vz, first, d, e, r.vys, r.vyr)
 
     def v_send(d):
-        to = rem(z + d, Z)
-        return send(lanes(r.val, to, HD), r.vz.at[seq], r.vs.at[d], r.vr.at[d], to * Y + y, dp)
+        return send(r.val.at[d], r.vz.at[seq], r.vs.at[d], r.vr.at[d], *zpeer(d))
 
     def pass_on(sent, via, d):
         sent(d).wait_recv()
         loop(1, Y, lambda e: via(None, d, e).start())
 
     k_mine = lanes(keys, z, HD)
-    v_mine = lanes(r.val, z, HD)
+    v_mine = r.val.at[Z]
     loop(1, Y, lambda e: k_forward(k_mine, 0, e).start())
     loop(1, Z, lambda d: pass_on(k_send, k_forward, d))
 
@@ -161,58 +160,58 @@
     get_weight.wait()
     own_h.wait()
     loop(1, PP, lambda d: h_send(d).wait_recv())
-    rows = X * TOK
-    width = min(512, kv)
-
-    def product(half):
-        block = r.cols[pl.ds(half * X, X)].reshape(rows, feat)
-
-        def piece(w):
-            r.part[aligned(half * rows, rows), aligned(w * width, width)] = jnp.dot(
-                block, r.weight[:, aligned(w * width, width)], preferred_element_type=F32
-            ).astype(BF16)
-
-        loop(0, kv // width, piece)
-
+    half = X * TOK
     other = 1 - c
 
     def c_send(i):
-        row = aligned((other * X + i) * TOK, TOK)
-        return send(r.part.at[row], r.pair.at[i], r.cs.at[i], r.cr.at[i], seq, sibling)
-
-    product(other)
-    loop(0, X, lambda i: c_send(i).start())
-    product(c)
-
-    def x_send(d):
+        src = r.part.at[i, aligned(other * half, half)]
+        return send(src, r.pair.at[i], r.cs.at[i], r.cr.at[i], seq, sibling)
+
+    def product(i):
+        head = rem(z + i, Z)
+        block = r.cols[...].reshape(PP * TOK, feat)
+        r.part[i] = jnp.dot(
+            block, r.weight[:, aligned(head * HD, HD)], preferred_element_type=F32
+        ).astype(BF16)
+        c_send(i).start()
+
+    loop(1, Z + 1, product)
+
+    def x_send(i, d):
         to = rem(x + d, X)
-        return send(r.both.at[to], r.xin.at[d], r.xs.at[d], r.xr.at[d], seq, to * C + c)
-
-    def join(d):
-        to = rem(x + d, X)
-        c_send(to).wait_recv()
-        mine = r.part[aligned((c * X + to) * TOK, TOK)].astype(F32)
-        r.both[to] = (mine + r.pair[to].astype(F32)).astype(BF16)
-
-    def join_send(d):
-        join(d)
-        x_send(d).start()
-
-    def join_all():
-        loop(1, X, join_send)
-        join(jnp.int32(X))
-
-    own_v = pltpu.make_async_copy(v_mine, r.vz.at[seq], r.loc.at[3])
-
-    def values_out():
-        total = r.both[x].astype(F32)
+        src = r.both.at[i, aligned(to * TOK, TOK)]
+        return send(src, r.xin.at[i, d], r.xs.at[i, d], r.xr.at[i, d], seq, to * C + c)
+
+    def join(i):
+        c_send(i).wait_recv()
+        mine = r.part[i, aligned(c * half, half)].astype(F32)
+        r.both[i] = (mine + r.pair[i].astype(F32)).astype(BF16)
+        loop(1, X, lambda d: x_send(i, d).start())
+
+    def values_out(i):
+        total = r.both[i, aligned(x * TOK, TOK)].astype(F32)
         for d in range(1, X):
-            x_send(d).wait_recv()
-            total = total + r.xin[d].astype(F32)
-        r.val[...] = total.astype(BF16)
-        loop(1, Z, lambda d: v_send(d).start())
-        own_v.start()
-        loop(1, Y, lambda e: v_forward(v_mine, 0, e).start())
+            x_send(i, d).wait_recv()
+            total = total + r.xin[i, d].astype(F32)
+        block = total.astype(BF16)
+        r.val[i] = block
+
+        @pl.when(i < Z)
+        def _():
+            v_send(i).start()
+
+        @pl.when(i == Z)
+        def _():
+            r.vz[seq] = block
+
+    def values_on(i):
+        @pl.when(i < Z)
+        def _():
+            pass_on(v_send, v_forward, i)
+
+        @pl.when(i == Z)
+        def _():
+            loop(1, Y, lambda e: v_forward(v_mine, i, e).start())
 
 
     own_k.wait()
@@ -254,36 +253,49 @@
         scale = 1.0 / jnp.sum(total, axis=0, keepdims=True)
         r.inverse[t] = jnp.broadcast_to(scale, (8, wide))
 
-    steps = {}
-    steps.setdefault(min(1, Z - 1), []).append(join_all)
-    steps.setdefault(min(3, Z - 1), []).append(values_out)
-
-    def score_step(d):
-        @pl.when(d > 0)
-        def _():
-            q_send(d).wait_recv()
-
-        weights_of(rem(z - d + Z, Z))
-        for at, calls in steps.items():
-
-            @pl.when(d == at)
-            def _(calls=calls):
-                for call in calls:
-                    call()
-
-    early = max(1, Z - 2)
-    loop(0, early, score_step)
-    if early <= 3 and Z - 1 >= early:
-        loop(early, Z, score_step)
-        loop(1, Z, lambda d: pass_on(v_send, v_forward, d))
-    else:
-        loop(1, Z, lambda d: pass_on(v_send, v_forward, d))
-        loop(early, Z, score_step)
+    values_stages = (join, values_out, values_on)
+
+    def front_tick(m):
+        for at, stage in enumerate(values_stages):
+
+            @pl.when((m >= at) & (m - at < Z // 2))
+            def _(at=at, stage=stage):
+                stage(2 * (m - at) + 1)
+                stage(2 * (m - at) + 2)
+
+        @pl.when((m > 0) & (m < Z))
+        def _():
+            q_send(m).wait_recv()
+
+        @pl.when(m < Z)
+        def _():
+            weights_of(rem(z - m + Z, Z))
+
+    loop(0, max(Z, Z // 2 + len(values_stages) - 1), front_tick)
+
+
+    def drain_front():
+        loop(1, Y, lambda e: k_forward(k_mine, 0, e).wait_send())
+        loop(1, Y, lambda e: v_forward(v_mine, Z, e).wait_send())
+        loop(1, PP, lambda d: h_send(d).wait_send())
+
+        def both_ways(i):
+            c_send(i).wait_send()
+            loop(1, X, lambda d: x_send(i, d).wait_send())
+
+        loop(1, Z + 1, both_ways)
+
+        def one(i):
+            loop(1, Y, lambda e: k_forward(None, i, e).wait_send())
+            loop(1, Y, lambda e: v_forward(None, i, e).wait_send())
+            for sent in (k_send, q_send, v_send):
+                sent(i).wait_send()
+
+        loop(1, Z, one)
 
 
     get_readout.wait()
-    own_v.wait()
-    loop(1, Y, lambda e: v_forward(v_mine, 0, e).wait_recv())
+    loop(1, Y, lambda e: v_forward(v_mine, Z, e).wait_recv())
     loop(1, Z, lambda d: loop(1, Y, lambda e: v_forward(None, d, e).wait_recv()))
 
     def turn(j):
@@ -347,6 +359,13 @@
 
     loop(0, Z, slope_step)
 
+    def drain_middle():
+        def one(i):
+            l_send(i).wait_send()
+            s_send(i).wait_send()
+
+        loop(1, Z, one)
+
 
     tokens = PP * TOK
     quarter = HD // Y
@@ -462,39 +481,44 @@
             z2(i).wait_recv()
             r.sum[...] += r.gr[i].astype(F32)
 
-    stages = (stage0, stage1, stage2, stage3, stage4, stage5, stage6)
+    def drain_last():
+        def one(i):
+            z1(i).wait_send()
+            z2(i).wait_send()
+
+        loop(1, Z, one)
+
+        def more(i):
+            loop(1, Y, lambda e: y1(i, e).wait_send())
+            loop(1, Y, lambda e: y2(i, e).wait_send())
+            loop(1, X, lambda d: xx(i, d).wait_send())
+            loop(0, X, lambda d: cc(i, d).wait_send())
+
+        loop(1, Z + 1, more)
+
+    stages = (
+        (11, stage6),
+        (9, stage5),
+        (7, stage4),
+        (6, stage3),
+        (4, stage2),
+        (2, stage1),
+        (0, stage0),
+    )
 
     def tick(k):
-        for s, stage in enumerate(stages):
-
-            @pl.when((k - s >= 1) & (k - s <= Z))
-            def _(s=s, stage=stage):
-                stage(k - s)
-
-    loop(1, Z + len(stages), tick)
+        for late, stage in stages:
+
+            @pl.when((k - late >= 1) & (k - late <= Z))
+            def _(late=late, stage=stage):
+                stage(k - late)
+
+    loop(1, Z + 1 + stages[0][0], tick)
     result[...] = r.sum[...] + r.own[...]
 
-
-    def drain(i):
-        loop(1, Y, lambda e: k_forward(None, i, e).wait_send())
-        loop(1, Y, lambda e: v_forward(None, i, e).wait_send())
-        for sent in (k_send, q_send, v_send, l_send, s_send, z1, z2):
-            sent(i).wait_send()
-
-    loop(1, Z, drain)
-    loop(1, Y, lambda e: k_forward(k_mine, 0, e).wait_send())
-    loop(1, Y, lambda e: v_forward(v_mine, 0, e).wait_send())
-    loop(1, PP, lambda d: h_send(d).wait_send())
-    loop(0, X, lambda i: c_send(i).wait_send())
-    loop(1, X, lambda d: x_send(d).wait_send())
-
-    def drain_late(i):
-        loop(1, Y, lambda e: y1(i, e).wait_send())
-        loop(1, Y, lambda e: y2(i, e).wait_send())
-        loop(1, X, lambda d: xx(i, d).wait_send())
-        loop(0, X, lambda d: cc(i, d).wait_send())
-
-    loop(1, Z + 1, drain_late)
+    drain_front()
+    drain_middle()
+    drain_last()
 
 
 def whole(n, hidden, queries, keys, weight, readout, base, labels, rows):
@@ -513,11 +537,11 @@
         qz=vmem((Z, TOK, qw), BF16),
         kz=vmem((n.S, TOK, HD), BF16),
         vz=vmem((n.S, TOK, HD), BF16),
-        part=vmem((PP * TOK, kv), BF16),
-        pair=vmem((X, TOK, kv), BF16),
-        both=vmem((X, TOK, kv), BF16),
-        xin=vmem((X, TOK, kv), BF16),
-        val=vmem((TOK, kv), BF16),
+        part=vmem((Z + 1, PP * TOK, HD), BF16),
+        pair=vmem((Z + 1, X * TOK, HD), BF16),
+        both=vmem((Z + 1, X * TOK, HD), BF16),
+        xin=vmem((Z + 1, X, TOK, HD), BF16),
+        val=vmem((Z + 1, TOK, HD), BF16),
         raw=vmem((Z * chunk, qw), F32),
         vt=vmem((Z, HD, chunk), BF16),
         out=vmem((HD, qw), F32),
@@ -544,13 +568,10 @@
         scratch |= {name + "s": dma((PP,)), name + "r": dma((PP,))}
     for name in ("k", "q", "v", "l", "s", "z1", "z2"):
         scratch |= {name + "s": dma((Z,)), name + "r": dma((Z,))}
-    for name in ("c", "x"):
-        scratch |= {name + "s": dma((X,)), name + "r": dma((X,))}
-    for name in ("ky", "vy"):
-        scratch |= {name + "s": dma((Z, Y)), name + "r": dma((Z, Y))}
-    for name in ("y1", "y2"):
+    scratch |= {"cs": dma((Z + 1,)), "cr": dma((Z + 1,))}
+    for name in ("ky", "vy", "y1", "y2"):
         scratch |= {name + "s": dma((Z + 1, Y)), name + "r": dma((Z + 1, Y))}
-    for name in ("x2", "c2"):
+    for name in ("x", "x2", "c2"):
         scratch |= {name + "s": dma((Z + 1, X)), name + "r": dma((Z + 1, X))}
     return pl.pallas_call(
         functools.partial(whole_kernel, n, tuple(scratch)),

time: 155 us -> 152 us (0.981); the launches traced: 155 us -> 150 us
  Pallas kernels: 153 us -> 148 us
    pallas_call x1, Pallas kernels: 153 us -> 148 us  [whole(): pl.pallas_call(functools.partial(whole_kernel, n, tuple(scratch)), out_sh...]
where the time goes in v3:
time: 152 us; the launch traced here: 150 us
  Pallas kernels  148 us (97%)
    pallas_call x1, Pallas kernels, whole(): pl.pallas_call(functools.partial(whole_kernel, n, tuple(scratch)), out_sh...  148 us

profile of v3, /device:TPU:1, one launch (start us, length us, event | category | flops | bytes accessed | tf_op | source)
XLA Modules:
  0.0 150.0 jit_solution(14403910983177841846)
XLA Ops:
  0.6 0.0 copy-start
  0.6 147.8 %whole.1 = f32[32,512]{1,0:T(8,128)} custom-call(bf16[128,4096]{1,0:T(8,128)(2,1)} %bitcast.4, bf16[128,4096]{1,0:T(8,128)(2,1)} %bitcast.5, bf16[128,1024]{1,0:T(8,128)(2,1)} %bitcast.6, bf16[512,1024]{1,0:T(8,128)(2,1)} %weight_in.1, bf16[4096,256]{1,0:T(8,128)(2,1)} %readout_in.1, f32[128,256]{1,0:T(8,128)} %bitcast.7, s32[1,128]{1,0:T(1,128)} %labels.1), custom_call_target="tpu_custom_call" | custom-call | tf_op jit(solution)/shard_map/whole/pallas_call | solution.py:576
  148.5 0.0 copy-done
  148.5 1.5 %multiply_add_fusion = (f32[32,512]{1,0:T(8,128)}, f32[32,512]{1,0:T(8,128)}) fusion(f32[32,512]{1,0:T(8,128)S(1)} %copy-done, f32[32,512]{1,0:T(8,128)} %whole.1), kind=kLoop, calls=%fused_computation | loop fusion | flops 81920 | bytes 262144 | tf_op jit(solution)/shard_map/add | solution.py:603
Async XLA Ops:
  0.6 147.8 %copy-start = (f32[32,512]{1,0:T(8,128)S(1)}, f32[32,512]{1,0:T(8,128)}, u32[]{:S(2)}) copy-start(f32[32,512]{1,0:T(8,128)} %param.15) | copy-start | bytes 196612

commit v4 on v3

--- a/solution.py
+++ b/solution.py
@@ -103,6 +103,10 @@
     def xpeer(d):
         return seq, rem(x + d, X) * C + c
 
+    def near(m):
+        odd = rem(m, 2)
+        return odd * ((m + 1) // 2) + (1 - odd) * rem(Z - m // 2, Z)
+
     def lanes(ref, i, width):
         return ref.at[:, aligned(i * width, width)]
 
@@ -131,7 +135,9 @@
 
     loop(1, Z, lambda d: k_send(d).start())
     loop(1, PP, lambda d: h_send(d).start())
-    loop(1, Z, lambda d: q_send(d).start())
+    q_first = min(Z, 5)
+    q_second = max(q_first, Z - 1)
+    loop(1, q_first, lambda m: q_send(near(m)).start())
 
     def forward(ref, first, d, e, ssem, rsem):
         at = rem(z - d + Z, Z) * Y + y
@@ -175,6 +181,7 @@
         ).astype(BF16)
         c_send(i).start()
 
+    loop(q_first, q_second, lambda m: q_send(near(m)).start())
     loop(1, Z + 1, product)
 
     def x_send(i, d):
@@ -263,15 +270,25 @@
                 stage(2 * (m - at) + 1)
                 stage(2 * (m - at) + 2)
 
-        @pl.when((m > 0) & (m < Z))
-        def _():
-            q_send(m).wait_recv()
+        @pl.when(m == Z // 2)
+        def _():
+            loop(q_second, Z, lambda i: q_send(near(i)).start())
 
         @pl.when(m < Z)
         def _():
-            weights_of(rem(z - m + Z, Z))
-
-    loop(0, max(Z, Z // 2 + len(values_stages) - 1), front_tick)
+            score_step(m)
+
+    def score_step(m):
+        d = near(m)
+
+        @pl.when(d > 0)
+        def _():
+            q_send(d).wait_recv()
+
+        weights_of(rem(z - d + Z, Z))
+
+    late = Z // 2 + len(values_stages) - 1
+    loop(0, late, front_tick)
 
 
     def drain_front():
@@ -308,7 +325,14 @@
         return send(r.share.at[to], r.arrived.at[d], r.ls.at[d], r.lr.at[d], to * Y + y, dp)
 
     def share_step(i):
-        t = rem(z + i, Z)
+        behind = late + i // 2 - 1
+
+        @pl.when((rem(i, 2) == 1) & (i > 1) & (behind < Z))
+        def _():
+            score_step(behind)
+
+        d = near(rem(i, Z))
+        t = rem(z - d + Z, Z)
         at = t * (t + 1) // 2
         r.out[...] = jnp.zeros_like(r.out)
 
@@ -323,12 +347,16 @@
             part = part + contract(mixed[:, at], r.readout[at, :], 0, 0)
         r.share[t] = part.astype(BF16)
 
-        @pl.when(i < Z)
-        def _():
-            l_send(i).start()
+        @pl.when(d > 0)
+        def _():
+            l_send(Z - d).start()
 
     loop(1, Z + 1, share_step)
 
+    def clear(j):
+        r.total[j] = jnp.zeros((chunk, HD), F32)
+
+    loop(0, Z, clear)
     total = base[...] + r.share[z].astype(F32)
     for d in range(1, Z):
         l_send(d).wait_recv()
@@ -343,9 +371,11 @@
     def s_send(d):
         return send(r.slopes.at[z], r.slopes.at[z], r.ss.at[d], r.sr.at[d], *zpeer(d))
 
-    loop(1, Z, lambda d: s_send(d).start())
-
-    def slope_step(d):
+    loop(1, Z, lambda m: s_send(near(m)).start())
+
+    def slope_step(m):
+        d = near(m)
+
         @pl.when(d > 0)
         def _():
             s_send(d).wait_recv()
@@ -355,7 +385,14 @@
         for h in range(group):
             at = slice(h * HD, (h + 1) * HD)
             column = r.inverse[t][:, at].T[:, :1]
-            r.d_rows[t, at, :] = (contract(slope, r.readout[at, :], 1, 1) * column).astype(BF16)
+            r.d_rows[at, :] = (contract(slope, r.readout[at, :], 1, 1) * column).astype(BF16)
+
+        def add(j):
+            r.total[j] += jnp.dot(
+                r.kept[t * (t + 1) // 2 + j], r.d_rows[...], preferred_element_type=F32
+            )
+
+        loop(0, t + 1, add)
 
     loop(0, Z, slope_step)
 
@@ -379,16 +416,8 @@
 
     def stage0(i):
         j = rem(z + i, Z)
-        r.acc[...] = jnp.zeros_like(r.acc)
-
-        def add(t):
-            r.acc[...] += jnp.dot(
-                r.kept[t * (t + 1) // 2 + j], r.d_rows[t], preferred_element_type=F32
-            )
-
-        loop(j, Z, add)
         for b in range(Y):
-            r.grads[i, b] = r.acc[b * TOK : (b + 1) * TOK, :].astype(BF16)
+            r.grads[i, b] = r.total[j, b * TOK : (b + 1) * TOK, :].astype(BF16)
         loop(1, Y, lambda e: y1(i, e).start())
 
     def z1(i):
@@ -497,14 +526,14 @@
         loop(1, Z + 1, more)
 
     stages = (
-        (11, stage6),
-        (9, stage5),
-        (7, stage4),
+        (14, stage6),
+        (11, stage5),
+        (8, stage4),
         (6, stage3),
-        (4, stage2),
-        (2, stage1),
-        (0, stage0),
+        (3, stage2),
+        (0, stage1),
     )
+    loop(1, Z + 1, stage0)
 
     def tick(k):
         for late, stage in stages:
@@ -550,8 +579,8 @@
         share=vmem((Z, TOK, cand), BF16),
         arrived=vmem((Z, TOK, cand), BF16),
         slopes=vmem((Z, TOK, cand), BF16),
-        d_rows=vmem((Z, qw, HD), BF16),
-        acc=vmem((chunk, HD), F32),
+        d_rows=vmem((qw, HD), BF16),
+        total=vmem((Z, chunk, HD), F32),
         grads=vmem((Z + 1, Y, TOK, HD), BF16),
         ya=vmem((Z + 1, Y, TOK, HD), BF16),
         dz=vmem((Z + 1, TOK, HD), BF16),

time: 152 us -> 145 us (0.954)
  Pallas kernels: 148 us -> 142 us
    pallas_call x1, Pallas kernels: 148 us -> 142 us  [whole(): pl.pallas_call(functools.partial(whole_kernel, n, tuple(scratch)), out_sh...]
where the time goes in v4:
time: 145 us; the launch traced here: 144 us
  Pallas kernels  142 us (98%)
  other arithmetic  1.51 us (1%)
    pallas_call x1, Pallas kernels, whole(): pl.pallas_call(functools.partial(whole_kernel, n, tuple(scratch)), out_sh...  142 us

profile of v4, /device:TPU:1, one launch (start us, length us, event | category | flops | bytes accessed | tf_op | source)
XLA Modules:
  0.0 144.3 jit_solution(10945330898809382381)
XLA Ops:
  0.6 0.0 copy-start
  0.6 142.1 %whole.1 = f32[32,512]{1,0:T(8,128)} custom-call(bf16[128,4096]{1,0:T(8,128)(2,1)} %bitcast.4, bf16[128,4096]{1,0:T(8,128)(2,1)} %bitcast.5, bf16[128,1024]{1,0:T(8,128)(2,1)} %bitcast.6, bf16[512,1024]{1,0:T(8,128)(2,1)} %weight_in.1, bf16[4096,256]{1,0:T(8,128)(2,1)} %readout_in.1, f32[128,256]{1,0:T(8,128)} %bitcast.7, s32[1,128]{1,0:T(1,128)} %labels.1), custom_call_target="tpu_custom_call" | custom-call | tf_op jit(solution)/shard_map/whole/pallas_call | solution.py:605
  142.8 0.0 copy-done
  142.8 1.5 %multiply_add_fusion = (f32[32,512]{1,0:T(8,128)}, f32[32,512]{1,0:T(8,128)}) fusion(f32[32,512]{1,0:T(8,128)S(1)} %copy-done, f32[32,512]{1,0:T(8,128)} %whole.1), kind=kLoop, calls=%fused_computation | loop fusion | flops 81920 | bytes 262144 | tf_op jit(solution)/shard_map/add | solution.py:632
Async XLA Ops:
  0.6 142.1 %copy-start = (f32[32,512]{1,0:T(8,128)S(1)}, f32[32,512]{1,0:T(8,128)}, u32[]{:S(2)}) copy-start(f32[32,512]{1,0:T(8,128)} %param.15) | copy-start | bytes 196612

commit v5 on v4

--- a/solution.py
+++ b/solution.py
@@ -220,6 +220,8 @@
         def _():
             loop(1, Y, lambda e: v_forward(v_mine, i, e).start())
 
+    loop(1, Z + 1, join)
+
 
     own_k.wait()
     own_q.wait()
@@ -260,10 +262,10 @@
         scale = 1.0 / jnp.sum(total, axis=0, keepdims=True)
         r.inverse[t] = jnp.broadcast_to(scale, (8, wide))
 
-    values_stages = (join, values_out, values_on)
+    values_stages = ((1, values_out), (3, values_on))
 
     def front_tick(m):
-        for at, stage in enumerate(values_stages):
+        for at, stage in values_stages:
 
             @pl.when((m >= at) & (m - at < Z // 2))
             def _(at=at, stage=stage):
@@ -287,8 +289,7 @@
 
         weights_of(rem(z - d + Z, Z))
 
-    late = Z // 2 + len(values_stages) - 1
-    loop(0, late, front_tick)
+    loop(0, max(Z, Z // 2 + values_stages[-1][0]), front_tick)
 
 
     def drain_front():
@@ -325,13 +326,7 @@
         return send(r.share.at[to], r.arrived.at[d], r.ls.at[d], r.lr.at[d], to * Y + y, dp)
 
     def share_step(i):
-        behind = late + i // 2 - 1
-
-        @pl.when((rem(i, 2) == 1) & (i > 1) & (behind < Z))
-        def _():
-            score_step(behind)
-
-        d = near(rem(i, Z))
+        d = near(Z - i)
         t = rem(z - d + Z, Z)
         at = t * (t + 1) // 2
         r.out[...] = jnp.zeros_like(r.out)
@@ -354,7 +349,7 @@
     loop(1, Z + 1, share_step)
 
     def clear(j):
-        r.total[j] = jnp.zeros((chunk, HD), F32)
+        r.total[j] = jnp.zeros((HD, chunk), F32)
 
     loop(0, Z, clear)
     total = base[...] + r.share[z].astype(F32)
@@ -384,13 +379,11 @@
         slope = r.slopes[t]
         for h in range(group):
             at = slice(h * HD, (h + 1) * HD)
-            column = r.inverse[t][:, at].T[:, :1]
-            r.d_rows[at, :] = (contract(slope, r.readout[at, :], 1, 1) * column).astype(BF16)
+            d_head = contract(r.readout[at, :], slope, 1, 1)
+            r.d_rows[:, at] = (d_head * r.inverse[t][:1, at]).astype(BF16)
 
         def add(j):
-            r.total[j] += jnp.dot(
-                r.kept[t * (t + 1) // 2 + j], r.d_rows[...], preferred_element_type=F32
-            )
+            r.total[j] += contract(r.d_rows[...], r.kept[t * (t + 1) // 2 + j], 1, 1)
 
         loop(0, t + 1, add)
 
@@ -417,7 +410,7 @@
     def stage0(i):
         j = rem(z + i, Z)
         for b in range(Y):
-            r.grads[i, b] = r.total[j, b * TOK : (b + 1) * TOK, :].astype(BF16)
+            r.grads[i, b] = r.total[j, :, b * TOK : (b + 1) * TOK].T.astype(BF16)
         loop(1, Y, lambda e: y1(i, e).start())
 
     def z1(i):
@@ -579,8 +572,8 @@
         share=vmem((Z, TOK, cand), BF16),
         arrived=vmem((Z, TOK, cand), BF16),
         slopes=vmem((Z, TOK, cand), BF16),
-        d_rows=vmem((qw, HD), BF16),
-        total=vmem((Z, chunk, HD), F32),
+        d_rows=vmem((HD, qw), BF16),
+        total=vmem((Z, HD, chunk), F32),
         grads=vmem((Z + 1, Y, TOK, HD), BF16),
         ya=vmem((Z + 1, Y, TOK, HD), BF16),
         dz=vmem((Z + 1, TOK, HD), BF16),

time: 145 us -> 136 us (0.938)
  Pallas kernels: 142 us -> 134 us
    pallas_call x1, Pallas kernels: 142 us -> 134 us  [whole(): pl.pallas_call(functools.partial(whole_kernel, n, tuple(scratch)), out_sh...]
where the time goes in v5:
time: 136 us
  Pallas kernels  134 us (99%)
  other arithmetic  1.51 us (1%)
    pallas_call x1, Pallas kernels, whole(): pl.pallas_call(functools.partial(whole_kernel, n, tuple(scratch)), out_sh...  134 us

profile of v5, /device:TPU:1, one launch (start us, length us, event | category | flops | bytes accessed | tf_op | source)
XLA Modules:
  0.0 136.3 jit_solution(9212768933980854278)
XLA Ops:
  0.6 0.0 copy-start
  0.6 134.2 %whole.1 = f32[32,512]{1,0:T(8,128)} custom-call(bf16[128,4096]{1,0:T(8,128)(2,1)} %bitcast.4, bf16[128,4096]{1,0:T(8,128)(2,1)} %bitcast.5, bf16[128,1024]{1,0:T(8,128)(2,1)} %bitcast.6, bf16[512,1024]{1,0:T(8,128)(2,1)} %weight_in.1, bf16[4096,256]{1,0:T(8,128)(2,1)} %readout_in.1, f32[128,256]{1,0:T(8,128)} %bitcast.7, s32[1,128]{1,0:T(1,128)} %labels.1), custom_call_target="tpu_custom_call" | custom-call | tf_op jit(solution)/shard_map/whole/pallas_call | solution.py:598
  134.8 0.0 copy-done
  134.8 1.5 %multiply_add_fusion = (f32[32,512]{1,0:T(8,128)}, f32[32,512]{1,0:T(8,128)}) fusion(f32[32,512]{1,0:T(8,128)S(1)} %copy-done, f32[32,512]{1,0:T(8,128)} %whole.1), kind=kLoop, calls=%fused_computation | loop fusion | flops 81920 | bytes 262144 | tf_op jit(solution)/shard_map/add | solution.py:625
Async XLA Ops:
  0.6 134.2 %copy-start = (f32[32,512]{1,0:T(8,128)S(1)}, f32[32,512]{1,0:T(8,128)}, u32[]{:S(2)}) copy-start(f32[32,512]{1,0:T(8,128)} %param.15) | copy-start | bytes 196612

commit v6 on v5

--- a/solution.py
+++ b/solution.py
@@ -364,16 +364,37 @@
     r.slopes[z] = (soft - jnp.where(label == column, 1.0, 0.0)).astype(BF16)
 
     def s_send(d):
-        return send(r.slopes.at[z], r.slopes.at[z], r.ss.at[d], r.sr.at[d], *zpeer(d))
-
-    loop(1, Z, lambda m: s_send(near(m)).start())
+        up = d <= Z // 2
+        at = jnp.where(up, rem(z - d + 1 + Z, Z), rem(z - d - 1 + 2 * Z, Z))
+        to = jnp.where(up, rem(z + 1, Z), rem(z - 1 + Z, Z))
+        ref = r.slopes.at[at]
+        return send(ref, ref, r.ss.at[d], r.sr.at[d], to * Y + y, dp)
+
+    s_send(jnp.int32(1)).start()
+    if Z > 2:
+        s_send(jnp.int32(Z - 1)).start()
+
+    def slopes_on(d):
+        s_send(d).wait_recv()
+
+        @pl.when(d < Z // 2)
+        def _():
+            s_send(d + 1).start()
+
+        @pl.when(d > Z // 2 + 1)
+        def _():
+            s_send(d - 1).start()
 
     def slope_step(m):
         d = near(m)
 
-        @pl.when(d > 0)
-        def _():
-            s_send(d).wait_recv()
+        @pl.when(rem(m, 2) == 1)
+        def _():
+            slopes_on(d)
+
+            @pl.when(m + 1 < Z)
+            def _():
+                slopes_on(Z - d)
 
         t = rem(z - d + Z, Z)
         slope = r.slopes[t]

time: 136 us -> 132 us (0.971)
  Pallas kernels: 134 us -> 130 us
    pallas_call x1, Pallas kernels: 134 us -> 130 us  [whole(): pl.pallas_call(functools.partial(whole_kernel, n, tuple(scratch)), out_sh...]
where the time goes in v6:
time: 132 us
  Pallas kernels  130 us (98%)
  other arithmetic  1.51 us (1%)
    pallas_call x1, Pallas kernels, whole(): pl.pallas_call(functools.partial(whole_kernel, n, tuple(scratch)), out_sh...  130 us

profile of v6, /device:TPU:1, one launch (start us, length us, event | category | flops | bytes accessed | tf_op | source)
XLA Modules:
  0.0 132.3 jit_solution(5022106406342059799)
XLA Ops:
  0.6 0.0 copy-start
  0.6 130.1 %whole.1 = f32[32,512]{1,0:T(8,128)} custom-call(bf16[128,4096]{1,0:T(8,128)(2,1)} %bitcast.4, bf16[128,4096]{1,0:T(8,128)(2,1)} %bitcast.5, bf16[128,1024]{1,0:T(8,128)(2,1)} %bitcast.6, bf16[512,1024]{1,0:T(8,128)(2,1)} %weight_in.1, bf16[4096,256]{1,0:T(8,128)(2,1)} %readout_in.1, f32[128,256]{1,0:T(8,128)} %bitcast.7, s32[1,128]{1,0:T(1,128)} %labels.1), custom_call_target="tpu_custom_call" | custom-call | tf_op jit(solution)/shard_map/whole/pallas_call | solution.py:619
  130.8 0.0 copy-done
  130.8 1.5 %multiply_add_fusion = (f32[32,512]{1,0:T(8,128)}, f32[32,512]{1,0:T(8,128)}) fusion(f32[32,512]{1,0:T(8,128)S(1)} %copy-done, f32[32,512]{1,0:T(8,128)} %whole.1), kind=kLoop, calls=%fused_computation | loop fusion | flops 81920 | bytes 262144 | tf_op jit(solution)/shard_map/add | solution.py:646
Async XLA Ops:
  0.6 130.2 %copy-start = (f32[32,512]{1,0:T(8,128)S(1)}, f32[32,512]{1,0:T(8,128)}, u32[]{:S(2)}) copy-start(f32[32,512]{1,0:T(8,128)} %param.15) | copy-start | bytes 196612
